TPU v7x, 128 devices: a whole 4x4x4 slice. The times are simulated.
128 devices in a mesh: px: 16 (over y, z_hi, core), py: 8 (over x, z_lo).
Axes of the slice: x: 4, y: 4, z: 4 (z_hi: 2, z_lo: 2; z = z_hi * 2 + z_lo), core: 2. Of those that a mesh axis runs over, the one named last changes fastest.
Arguments:
- level_set: float32 [256, 128, 1024], P('px', 'py'), may hold values from -6 to 6
- flow_amplitude: float32 [3], replicated, may hold values from 0.1 to 0.25
Outputs:
- phi_next: float32 [256, 128, 1024], P('px', 'py')
- vertices: float32 [3, 256, 128, 1024], P(None, 'px', None, 'py')
All inputs are finite; a program needn't handle non-finite values.
Results may differ from a plain program's by a relative error of at most 0.0003.
Values sent between devices are 32-bit elements; how exact they have to be, the bound alone decides.
No kernel may reach another device: no remote copies, remote signals or barrier semaphores. Data moves between devices by JAX's collectives and lax.ppermute only.
A program may use at most 64 MiB of HBM per device.

v0:
```python
import jax
import jax.numpy as jnp
from jax import lax
from jax.sharding import PartitionSpec as P

weno_eps = 1e-06
sharpness = 4.0
crossing_bias = 0.05
mass_prior = 0.05
tikhonov = 0.25
pseudo_step = 0.5
gradient_eps = 1e-06


def padded_2(x, sides, width):
    edges = {}
    for axis, dim in sides:
        count, length = (lax.axis_size(axis), x.shape[dim])
        up = [(i, (i + 1) % count) for i in range(count - 1)]
        last = lax.slice_in_dim(x, length - width, length, axis=dim)
        leading = lax.slice_in_dim(x, 0, width, axis=dim)
        edges[dim] = (
            lax.ppermute(last, axis, up),
            lax.ppermute(leading, axis, [(b, a) for a, b in up]),
        )
    done = []
    for _, dim in sides:
        low, high = edges[dim]
        around = [(width, width) if d in done else (0, 0) for d in range(x.ndim)]
        x = jnp.concatenate([jnp.pad(low, around), x, jnp.pad(high, around)], axis=dim)
        done.append(dim)
    return x


def cut_along(x, dim, count):
    before, after = (x.shape[:dim], x.shape[dim + 1 :])
    return jnp.moveaxis(x.reshape(*before, count, -1, *after), dim, 0)


def piece_ends(length, count):
    unit = 8 if length >= 8 * count else 1
    return [length // unit * k // count * unit for k in range(1, count)]


def joined_along(parts, dim):
    dims = list(parts.shape[1:])
    dims[dim] *= parts.shape[0]
    return jnp.moveaxis(parts, 0, dim).reshape(dims)


def several_exchanges(x, axis, pieces, split_dim, concat_dim):
    parts = cut_along(x, split_dim, lax.axis_size(axis))
    widest = max(range(1, max(2, parts.ndim - 1)), key=lambda d: parts.shape[d])
    gathered = []
    for share in jnp.split(parts, piece_ends(parts.shape[widest], pieces), axis=widest):
        if share.size:
            gathered.append(lax.all_to_all(share, axis, split_axis=0, concat_axis=0, tiled=True))
    return joined_along(jnp.concatenate(gathered, axis=widest), concat_dim)


def from_behind(value, axis, steps):
    count = lax.axis_size(axis)
    leading, last = (max(0, -steps), min(count, count - steps))
    return lax.ppermute(value, axis, [(source, source + steps) for source in range(leading, last)])


def weno_side(delta_one, delta_two, delta_three, delta_four, delta_five):
    guess_one = delta_one / 3.0 - 7.0 * delta_two / 6.0 + 11.0 * delta_three / 6.0
    guess_two = -delta_two / 6.0 + 5.0 * delta_three / 6.0 + delta_four / 3.0
    guess_three = delta_three / 3.0 + 5.0 * delta_four / 6.0 - delta_five / 6.0
    smooth_one = (
        13.0 / 12.0 * (delta_one - 2.0 * delta_two + delta_three) ** 2
        + 0.25 * (delta_one - 4.0 * delta_two + 3.0 * delta_three) ** 2
    )
    smooth_two = (
        13.0 / 12.0 * (delta_two - 2.0 * delta_three + delta_four) ** 2
        + 0.25 * (delta_two - delta_four) ** 2
    )
    smooth_three = (
        13.0 / 12.0 * (delta_three - 2.0 * delta_four + delta_five) ** 2
        + 0.25 * (3.0 * delta_three - 4.0 * delta_four + delta_five) ** 2
    )
    weight_one = 0.1 / (smooth_one + weno_eps) ** 2
    weight_two = 0.6 / (smooth_two + weno_eps) ** 2
    weight_three = 0.3 / (smooth_three + weno_eps) ** 2
    return (weight_one * guess_one + weight_two * guess_two + weight_three * guess_three) / (
        weight_one + weight_two + weight_three
    )


def upwind_pair(padded, dimension, length):
    deltas = lax.slice_in_dim(padded, 1, length + 6, axis=dimension) - lax.slice_in_dim(
        padded, 0, length + 5, axis=dimension
    )
    window = [
        lax.slice_in_dim(deltas, offset, offset + length, axis=dimension) for offset in range(6)
    ]
    left_side = weno_side(window[0], window[1], window[2], window[3], window[4])
    right_side = weno_side(window[5], window[4], window[3], window[2], window[1])
    return (left_side, right_side)


def flow_block(
    flow_amplitude, x_start, y_start, row_count, col_count, layer_count, total_x, total_y, total_z
):
    x_cells = (
        (x_start + jnp.arange(row_count, dtype=jnp.int32)).astype(jnp.float32) + 0.5
    ) / total_x
    y_cells = (
        (y_start + jnp.arange(col_count, dtype=jnp.int32)).astype(jnp.float32) + 0.5
    ) / total_y
    z_cells = (jnp.arange(layer_count, dtype=jnp.int32).astype(jnp.float32) + 0.5) / total_z
    half_x = jnp.sin(jnp.pi * x_cells) ** 2
    half_y = jnp.sin(jnp.pi * y_cells) ** 2
    half_z = jnp.sin(jnp.pi * z_cells) ** 2
    full_x = jnp.sin(2.0 * jnp.pi * x_cells)
    full_y = jnp.sin(2.0 * jnp.pi * y_cells)
    full_z = jnp.sin(2.0 * jnp.pi * z_cells)
    speed_x = (
        2.0
        * flow_amplitude[0]
        * half_x[:, None, None]
        * full_y[None, :, None]
        * full_z[None, None, :]
    )
    speed_y = (
        -flow_amplitude[1] * full_x[:, None, None] * half_y[None, :, None] * full_z[None, None, :]
    )
    speed_z = (
        -flow_amplitude[2] * full_x[:, None, None] * full_y[None, :, None] * half_z[None, None, :]
    )
    return (speed_x, speed_y, speed_z)


def combine_rate(velocity, x_pair, y_pair, z_pair):
    speed_x, speed_y, speed_z = velocity
    advection = speed_x * jnp.where(speed_x > 0, x_pair[0], x_pair[1])
    advection = advection + speed_y * jnp.where(speed_y > 0, y_pair[0], y_pair[1])
    advection = advection + speed_z * jnp.where(speed_z > 0, z_pair[0], z_pair[1])
    return -advection


def advect_rate(padded, velocity):
    row_count = padded.shape[0] - 6
    col_count = padded.shape[1] - 6
    centre = padded[3 : 3 + row_count, 3 : 3 + col_count, :]
    x_pair = upwind_pair(padded[:, 3 : 3 + col_count, :], 0, row_count)
    y_pair = upwind_pair(padded[3 : 3 + row_count, :, :], 1, col_count)
    z_padded = jnp.pad(centre, ((0, 0), (0, 0), (3, 3)), mode="edge")
    z_pair = upwind_pair(z_padded, 2, centre.shape[2])
    return combine_rate(velocity, x_pair, y_pair, z_pair)


def godunov_parts(centre, behind, forward):
    positive = centre > 0
    growing = jnp.maximum(jnp.maximum(behind, 0.0) ** 2, jnp.minimum(forward, 0.0) ** 2)
    falling = jnp.maximum(jnp.minimum(behind, 0.0) ** 2, jnp.maximum(forward, 0.0) ** 2)
    return jnp.where(positive, growing, falling)


def finish_sweep(centre, x_part, y_part, z_part):
    smooth_sign = centre / jnp.sqrt(centre * centre + 1.0)
    magnitude = jnp.sqrt(x_part + y_part + z_part + gradient_eps)
    return centre - pseudo_step * smooth_sign * (magnitude - 1.0)


def reinit_sweep(padded):
    centre = padded[1:-1, 1:-1, :]
    x_part = godunov_parts(centre, centre - padded[:-2, 1:-1, :], padded[2:, 1:-1, :] - centre)
    y_part = godunov_parts(centre, centre - padded[1:-1, :-2, :], padded[1:-1, 2:, :] - centre)
    z_padded = jnp.pad(centre, ((0, 0), (0, 0), (1, 1)), mode="edge")
    z_part = godunov_parts(centre, centre - z_padded[:, :, :-2], z_padded[:, :, 2:] - centre)
    return finish_sweep(centre, x_part, y_part, z_part)


def set_bit(corner_key, direction, value):
    listed = list(corner_key)
    listed[direction] = value
    return tuple(listed)


def contour(spread, upper_plane):
    row_count = spread.shape[0] - 1
    col_count = spread.shape[1] - 1
    raised_z = jnp.concatenate([spread[:, :, 1:], upper_plane], axis=2)
    corners = {}
    for bit_x in (0, 1):
        for bit_y in (0, 1):
            corners[bit_x, bit_y, 0] = spread[
                bit_x : bit_x + row_count, bit_y : bit_y + col_count, :
            ]
            corners[bit_x, bit_y, 1] = raised_z[
                bit_x : bit_x + row_count, bit_y : bit_y + col_count, :
            ]
    ordered = sorted(corners)
    differences = {}
    for direction in range(3):
        for corner_key in ordered:
            if corner_key[direction] == 0:
                differences[direction, corner_key] = (
                    corners[set_bit(corner_key, direction, 1)] - corners[corner_key]
                )
    empty_sum = jnp.zeros_like(corners[0, 0, 0])
    weight_sum = empty_sum
    mass_sum = [empty_sum, empty_sum, empty_sum]
    index_pairs = ((0, 0), (0, 1), (0, 2), (1, 1), (1, 2), (2, 2))
    moment = {index_pair: empty_sum for index_pair in index_pairs}
    target = [empty_sum, empty_sum, empty_sum]
    for direction in range(3):
        for corner_key in ordered:
            if corner_key[direction] != 0:
                continue
            value_low = corners[corner_key]
            value_high = corners[set_bit(corner_key, direction, 1)]
            weight = jax.nn.sigmoid(-sharpness * value_low * value_high)
            low_square = value_low * value_low
            fraction = (low_square + crossing_bias) / (
                low_square + value_high * value_high + 2.0 * crossing_bias
            )
            normal = [None, None, None]
            normal[direction] = differences[direction, corner_key]
            for across in range(3):
                if across != direction:
                    start_key = set_bit(corner_key, across, 0)
                    end_key = set_bit(start_key, direction, 1)
                    normal[across] = (1.0 - fraction) * differences[
                        across, start_key
                    ] + fraction * differences[across, end_key]
            projection = normal[direction] * fraction
            for across in range(3):
                if across != direction and corner_key[across] == 1:
                    projection = projection + normal[across]
            weight_sum = weight_sum + weight
            mass_sum[direction] = mass_sum[direction] + weight * fraction
            for across in range(3):
                if across != direction and corner_key[across] == 1:
                    mass_sum[across] = mass_sum[across] + weight
            for index_pair in index_pairs:
                moment[index_pair] = (
                    moment[index_pair] + weight * normal[index_pair[0]] * normal[index_pair[1]]
                )
            weighted = weight * projection
            for across in range(3):
                target[across] = target[across] + weighted * normal[across]
    right_hand = [
        target[across]
        + tikhonov * ((mass_sum[across] + 0.5 * mass_prior) / (weight_sum + mass_prior))
        for across in range(3)
    ]
    system = {}
    for index_pair in index_pairs:
        system[index_pair] = (
            moment[index_pair] + tikhonov if index_pair[0] == index_pair[1] else moment[index_pair]
        )
    cofactor = {}
    cofactor[0, 0] = system[1, 1] * system[2, 2] - system[1, 2] * system[1, 2]
    cofactor[0, 1] = system[0, 2] * system[1, 2] - system[0, 1] * system[2, 2]
    cofactor[0, 2] = system[0, 1] * system[1, 2] - system[0, 2] * system[1, 1]
    cofactor[1, 1] = system[0, 0] * system[2, 2] - system[0, 2] * system[0, 2]
    cofactor[1, 2] = system[0, 1] * system[0, 2] - system[0, 0] * system[1, 2]
    cofactor[2, 2] = system[0, 0] * system[1, 1] - system[0, 1] * system[0, 1]
    determinant = (
        system[0, 0] * cofactor[0, 0]
        + system[0, 1] * cofactor[0, 1]
        + system[0, 2] * cofactor[0, 2]
    )
    solve_x = (
        cofactor[0, 0] * right_hand[0]
        + cofactor[0, 1] * right_hand[1]
        + cofactor[0, 2] * right_hand[2]
    ) / determinant
    solve_y = (
        cofactor[0, 1] * right_hand[0]
        + cofactor[1, 1] * right_hand[1]
        + cofactor[1, 2] * right_hand[2]
    ) / determinant
    solve_z = (
        cofactor[0, 2] * right_hand[0]
        + cofactor[1, 2] * right_hand[1]
        + cofactor[2, 2] * right_hand[2]
    ) / determinant
    return jnp.stack([solve_x, solve_y, solve_z])


def edge_fill(values, margin, first_x, last_x, first_y, last_y, second):
    row_total = values.shape[0]
    rows_at = jnp.arange(row_total)[:, None, None]
    values = jnp.where(first_x & (rows_at < margin), values[margin : margin + 1], values)
    values = jnp.where(
        last_x & (rows_at >= row_total - margin),
        values[row_total - margin - 1 : row_total - margin],
        values,
    )
    other_total = values.shape[second]
    shape_list = [1, 1, 1]
    shape_list[second] = other_total
    other_at = jnp.arange(other_total).reshape(shape_list)
    low_plane = lax.slice_in_dim(values, margin, margin + 1, axis=second)
    high_plane = lax.slice_in_dim(
        values, other_total - margin - 1, other_total - margin, axis=second
    )
    values = jnp.where(first_y & (other_at < margin), low_plane, values)
    values = jnp.where(last_y & (other_at >= other_total - margin), high_plane, values)
    return values


def shards(level_set, flow_amplitude):
    row_count, col_count, layer_count = level_set.shape
    index_x = lax.axis_index("px")
    index_y = lax.axis_index("py")
    count_x = lax.axis_size("px")
    count_y = lax.axis_size("py")
    total_x = row_count * count_x
    total_y = col_count * count_y
    first_x = index_x == 0
    last_x = index_x == count_x - 1
    first_y = index_y == 0
    last_y = index_y == count_y - 1
    velocity = flow_block(
        flow_amplitude,
        index_x * row_count,
        index_y * col_count,
        row_count,
        col_count,
        layer_count,
        total_x,
        total_y,
        layer_count,
    )

    def widened(field, width):
        extended = padded_2(field, (("px", 0), ("py", 1)), width)
        return edge_fill(extended, width, first_x, last_x, first_y, last_y, 1)

    phi_one = level_set + advect_rate(widened(level_set, 3), velocity)
    phi_two = 0.75 * level_set + 0.25 * (phi_one + advect_rate(widened(phi_one, 3), velocity))
    phi_three = 1.0 / 3.0 * level_set + 2.0 / 3.0 * (
        phi_two + advect_rate(widened(phi_two, 3), velocity)
    )
    phi_next = reinit_sweep(widened(phi_three, 1))
    brick_block = several_exchanges(phi_next, "py", 2, 2, 1)
    face_x = from_behind(brick_block[0:1], "px", -1)
    face_x = jnp.where(last_x, brick_block[row_count - 1 :], face_x)
    spread = jnp.concatenate([brick_block, face_x], axis=0)
    spread = jnp.concatenate([spread, spread[:, spread.shape[1] - 1 :]], axis=1)
    face_z = from_behind(spread[:, :, 0:1], "py", -1)
    face_z = jnp.where(last_y, spread[:, :, spread.shape[2] - 1 :], face_z)
    vertices = contour(spread, face_z)
    return (phi_next, vertices)


def solution(mesh):
    in_specs = (P("px", "py", None), P())
    out_specs = (P("px", "py", None), P(None, "px", None, "py"))
    return jax.shard_map(shards, mesh=mesh, in_specs=in_specs, out_specs=out_specs, check_vma=False)
```

profile of v0, /device:TPU:9, one launch (start us, length us, event | category | flops | bytes accessed | tf_op | source)
XLA Modules:
  0.0 238.5 jit_solution(2045314665452082159)
XLA Ops:
  2.5 3.6 %collective-permute-start = (f32[16,3,1024]{2,0,1:T(8,128)S(1)}, f32[16,3,1024]{2,0,1:T(8,128)S(1)}, u32[]{:S(2)}, u32[]{:S(2)}) collective-permute-start(f32[16,3,1024]{2,0,1:T(8,128)S(1)} %get-tuple-element.112), channel_id=1, source_target_pairs={{0,1},{1,2},{2,3},{3,4},{4,5},{5,6},{6,7},{8,9},{9,10},{10,11},{11... | collective-permute-start | bytes 589832 | tf_op jit(solution)/shard_map/ppermute | solution.py:23
  7.5 6.1 %collective-permute-start.1 = (f32[3,16,1024]{2,0,1:T(4,128)S(1)}, f32[3,16,1024]{2,0,1:T(4,128)S(1)}, u32[]{:S(2)}, u32[]{:S(2)}) collective-permute-start(f32[3,16,1024]{2,0,1:T(4,128)S(1)} %get-tuple-element.110), channel_id=1, source_target_pairs={{0,8},{8,16},{16,24},{24,32},{32,40},{40,48},{48,56},{56,64},{64,7... | collective-permute-start | bytes 589832 | tf_op jit(solution)/shard_map/ppermute | solution.py:23
  18.4 6.0 %collective-permute-done.2 = f32[3,16,1024]{2,0,1:T(4,128)S(1)} collective-permute-done((f32[3,16,1024]{2,0,1:T(4,128)S(1)}, f32[3,16,1024]{2,0,1:T(4,128)S(1)}, u32[]{:S(2)}, u32[]{:S(2)}) %collective-permute-start.2) | collective-permute-done | bytes 196640 | tf_op jit(solution)/shard_map/ppermute | solution.py:24
  34.1 14.9 %fusion.29 = f32[16,16,1024]{2,0,1:T(8,128)S(1)} fusion(f32[16,16,1029]{2,0,1:T(8,128)S(1)} %slice_subtract_fusion.8, f32[16,21,1024]{2,0,1:T(8,128)S(1)} %slice_subtract_fusion.5, f32[21,16,1024]{2,0,1:T(8,128)S(1)} %copy-done.1, f32[1024]{0:T(1024)S(1)} %get-tuple-element.125, f32[16,16]{0,1:T(8,128)S(1)} %get-tuple-element.115, ...), kind=kLoop, calls=%fused_computation.95 | loop fusion | flops 101711872 | bytes 20982784 | tf_op jit(solution)/shard_map/add | solution.py:335
  52.5 2.6 %collective-permute-start.5 = (f32[3,16,1024]{2,0,1:T(4,128)S(1)}, f32[3,16,1024]{2,0,1:T(4,128)S(1)}, u32[]{:S(2)}, u32[]{:S(2)}) collective-permute-start(f32[3,16,1024]{2,0,1:T(4,128)S(1)} %get-tuple-element.106), channel_id=1, source_target_pairs={{0,8},{8,16},{16,24},{24,32},{32,40},{40,48},{48,56},{56,64},{64,7... | collective-permute-start | bytes 589832 | tf_op jit(solution)/shard_map/ppermute | solution.py:23
  55.1 2.1 collective-permute-start.6
  59.0 5.9 %collective-permute-done.5 = f32[3,16,1024]{2,0,1:T(4,128)S(1)} collective-permute-done((f32[3,16,1024]{2,0,1:T(4,128)S(1)}, f32[3,16,1024]{2,0,1:T(4,128)S(1)}, u32[]{:S(2)}, u32[]{:S(2)}) %collective-permute-start.5) | collective-permute-done | bytes 196640 | tf_op jit(solution)/shard_map/ppermute | solution.py:23
  64.9 2.9 %collective-permute-done.6 = f32[3,16,1024]{2,0,1:T(4,128)S(1)} collective-permute-done((f32[3,16,1024]{2,0,1:T(4,128)S(1)}, f32[3,16,1024]{2,0,1:T(4,128)S(1)}, u32[]{:S(2)}, u32[]{:S(2)}) %collective-permute-start.6) | collective-permute-done | bytes 196640 | tf_op jit(solution)/shard_map/ppermute | solution.py:24
  77.0 2.2 concatenate.59
  79.2 2.1 slice_subtract_fusion.7
  81.6 15.0 %fusion.35 = f32[16,16,1024]{2,0,1:T(8,128)S(1)} fusion(f32[16,16,1024]{2,0,1:T(8,128)S(1)} %fusion.29, f32[16,16,1029]{2,0,1:T(8,128)S(1)} %slice_subtract_fusion.7, f32[16,21,1024]{2,0,1:T(8,128)S(1)} %slice_subtract_fusion.4, f32[21,16,1024]{2,0,1:T(8,128)S(1)} %copy-done.2, f32[1024]{0:T(1024)S(1)} %get-tuple-element.125, ...), kind=kLoop, calls=%fused_computation.101 | loop fusion | flops 102498304 | bytes 22031360 | tf_op jit(solution)/shard_map/add | solution.py:336
  99.3 3.0 %collective-permute-start.9 = (f32[3,16,1024]{2,0,1:T(4,128)S(1)}, f32[3,16,1024]{2,0,1:T(4,128)S(1)}, u32[]{:S(2)}, u32[]{:S(2)}) collective-permute-start(f32[3,16,1024]{2,0,1:T(4,128)S(1)} %get-tuple-element.102), channel_id=1, source_target_pairs={{0,8},{8,16},{16,24},{24,32},{32,40},{40,48},{48,56},{56,64},{64,7... | collective-permute-start | bytes 589832 | tf_op jit(solution)/shard_map/ppermute | solution.py:23
  102.3 2.1 collective-permute-start.10
  104.5 2.5 %collective-permute-done.11 = f32[16,3,1024]{2,0,1:T(8,128)S(1)} collective-permute-done((f32[16,3,1024]{2,0,1:T(8,128)S(1)}, f32[16,3,1024]{2,0,1:T(8,128)S(1)}, u32[]{:S(2)}, u32[]{:S(2)}) %collective-permute-start.11) | collective-permute-done | bytes 196640 | tf_op jit(solution)/shard_map/ppermute | solution.py:24
  106.9 5.7 %collective-permute-done.9 = f32[3,16,1024]{2,0,1:T(4,128)S(1)} collective-permute-done((f32[3,16,1024]{2,0,1:T(4,128)S(1)}, f32[3,16,1024]{2,0,1:T(4,128)S(1)}, u32[]{:S(2)}, u32[]{:S(2)}) %collective-permute-start.9) | collective-permute-done | bytes 196640 | tf_op jit(solution)/shard_map/ppermute | solution.py:23
  123.5 2.2 concatenate.62
  125.7 2.1 slice_subtract_fusion.6
  128.1 15.0 %fusion.41 = f32[16,16,1024]{2,0,1:T(8,128)S(1)} fusion(f32[16,16,1024]{2,0,1:T(8,128)S(1)} %fusion.35, f32[16,16,1029]{2,0,1:T(8,128)S(1)} %slice_subtract_fusion.6, f32[16,21,1024]{2,0,1:T(8,128)S(1)} %slice_subtract_fusion.3, f32[21,16,1024]{2,0,1:T(8,128)S(1)} %copy-done, f32[1024]{0:T(1024)S(1)} %get-tuple-element.125, ...), kind=kLoop, calls=%fused_computation.107 | loop fusion | flops 102498304 | bytes 22031360 | tf_op jit(solution)/shard_map/add | solution.py:337
  143.2 4.1 %collective-permute-start.13 = (f32[1,16,1024]{2,0,1:T(1,128)S(1)}, f32[1,16,1024]{2,0,1:T(1,128)S(1)}, u32[]{:S(2)}, u32[]{:S(2)}) collective-permute-start(f32[1,16,1024]{2,0,1:T(1,128)S(1)} %get-tuple-element.98), channel_id=1, source_target_pairs={{0,8},{8,16},{16,24},{24,32},{32,40},{40,48},{48,56},{56,64},{64,7... | collective-permute-start | bytes 196616 | tf_op jit(solution)/shard_map/ppermute | solution.py:23
  151.9 3.1 %collective-permute-done.14 = f32[1,16,1024]{2,0,1:T(1,128)S(1)} collective-permute-done((f32[1,16,1024]{2,0,1:T(1,128)S(1)}, f32[1,16,1024]{2,0,1:T(1,128)S(1)}, u32[]{:S(2)}, u32[]{:S(2)}) %collective-permute-start.14) | collective-permute-done | bytes 65568 | tf_op jit(solution)/shard_map/ppermute | solution.py:24
  159.2 2.5 %multiply_subtract_fusion.4 = f32[16,16,1024]{2,0,1:T(8,128)S(1)} fusion(f32[16,16,1024]{2,0,1:T(8,128)S(1)} %slice.723, f32[16,16,1]{2,0,1:T(8,128)S(1)} %get-tuple-element.80, f32[16,16,1]{2,0,1:T(8,128)S(1)} %get-tuple-element.79, f32[18,18,1024]{2,0,1:T(8,128)S(1)} %select_select_fusion.3), kind=kLoop, calls=%fused_computation.197 | loop fusion | flops 13631488 | bytes 6293504 | tf_op jit(solution)/shard_map/sub | solution.py:164
  162.6 12.4 %all_to_all.10 = f32[8,8,16,128]{3,1,2,0:T(8,128)S(1)} all-to-all(f32[8,8,16,128]{3,1,2,0:T(8,128)S(1)} %get-tuple-element.97), channel_id=1, replica_groups=mesh['px'=16,'py'=8] {'py'}, dimensions={0} | all-to-all | bytes 1048576 | tf_op jit(solution)/shard_map/all_to_all | solution.py:57
  175.0 3.5 %all-to-all-start.1 = ((f32[8,8,16,128]{3,1,2,0:T(8,128)}), f32[8,8,16,128]{3,1,2,0:T(8,128)S(1)}, u32[]{:S(2)}, u32[]{:S(2)}) async-start(f32[8,8,16,128]{3,1,2,0:T(8,128)} %get-tuple-element.96), calls=%async_computation.1 | async-start | bytes 1048576 | tf_op jit(solution)/shard_map/all_to_all | solution.py:57
  178.6 6.9 %all-to-all-done.1 = f32[8,8,16,128]{3,1,2,0:T(8,128)S(1)} async-done(((f32[8,8,16,128]{3,1,2,0:T(8,128)}), f32[8,8,16,128]{3,1,2,0:T(8,128)S(1)}, u32[]{:S(2)}, u32[]{:S(2)}) %all-to-all-start.1) | async-done | bytes 524320 | tf_op jit(solution)/shard_map/all_to_all | solution.py:57
  185.7 7.5 %collective-permute-start.16 = (f32[1,128,128]{1,2,0:T(8,128)S(1)}, f32[1,128,128]{1,2,0:T(8,128)S(1)}, u32[]{:S(2)}, u32[]{:S(2)}) collective-permute-start(f32[1,128,128]{1,2,0:T(8,128)S(1)} %copy.51), channel_id=1, source_target_pairs={{8,0},{16,8},{24,16},{32,24},{40,32},{48,40},{56,48},{64,56},{72,6... | collective-permute-start | bytes 196616 | tf_op jit(solution)/shard_map/ppermute | solution.py:64
  199.3 2.7 %collective-permute-done.17 = f32[17,129,1]{1,2,0:T(1,128)S(1)} collective-permute-done((f32[17,129,1]{1,2,0:T(1,128)S(1)}, f32[17,129,1]{1,2,0:T(1,128)S(1)}, u32[]{:S(2)}, u32[]{:S(2)}) %collective-permute-start.17) | collective-permute-done | bytes 8804 | tf_op jit(solution)/shard_map/ppermute | solution.py:64
  203.3 2.9 %add_divide_fusion.2 = (f32[16,128,128]{1,2,0:T(8,128)}, f32[16,128,128]{1,2,0:T(8,128)S(1)}, f32[16,128,128]{1,2,0:T(8,128)}, f32[16,128,128]{1,2,0:T(8,128)S(1...) fusion(f32[16,128,128]{1,2,0:T(8,128)S(1)} %get-tuple-element.19, f32[17,129,1]{1,2,0:T(1,128)S(1)} %broadcast_select_fusion.8, ...), kind=kLoop, calls=%fused_computation.159 | loop fusion | flops 5767168 | bytes 9511424 | tf_op jit(solution)/shard_map/div | solution.py:217
  207.8 2.6 %slice_subtract_fusion.17 = (f32[16,128,128]{1,2,0:T(8,128)S(1)}, f32[16,128,128]{1,2,0:T(8,128)S(1)}, f32[16,128,128]{1,2,0:T(8,128)S(1)}, f32[16,128,128]{1,2,...) fusion(f32[16,128,128]{1,2,0:T(8,128)S(1)} %copy.50, ...), kind=kLoop, calls=%fused_computation.210 | loop fusion | flops 13893632 | bytes 20971520 | tf_op jit(solution)/shard_map/sub | solution.py:201
  210.3 3.3 %fusion.63 = (f32[16,128,128]{1,2,0:T(8,128)S(1)}, f32[16,128,128]{1,2,0:T(8,128)S(1)}, f32[16,128,128]{1,2,0:T(8,128)S(1)}, f32[16,128,128]{1,2,0:T(8,128)S(1)}...) fusion(f32[16,128,128]{1,2,0:T(8,128)S(1)} %get-tuple-element.4, ...), kind=kLoop, calls=%fused_computation.260 | loop fusion | flops 12058624 | bytes 19922944 | tf_op jit(solution)/shard_map/sub | solution.py:201
  213.7 19.1 %divide_bitcast_fusion.2 = (f32[1,16,128,128]{2,3,1,0:T(8,128)S(1)}, f32[16,128,128]{1,2,0:T(8,128)S(1)}, f32[16,128,128]{1,2,0:T(8,128)S(1)}, f32[16,128,128]{1...) fusion(f32[16,128,128]{1,2,0:T(8,128)S(1)} %get-tuple-element.4, ...), kind=kLoop, calls=%fused_computation.121 | loop fusion | flops 116129792 | bytes 48234496 | tf_op jit(solution)/shard_map/stack | solution.py:282
  232.8 3.1 %divide_bitcast_fusion.1 = (f32[1,16,128,128]{2,3,1,0:T(8,128)S(1)}, f32[1,16,128,128]{2,3,1,0:T(8,128)S(1)}) fusion(f32[16,128,128]{1,2,0:T(8,128)} %get-tuple-element.15, f32[16,128,128]{1,2,0:T(8,128)S(1)} %get-tuple-element.11, f32[16,128,128]{1,2,0:T(8,128)S(1)} %get-tuple-element.8, f32[16,128,128]{1,2,0:T(8,128)} %get-tuple-element.13, ...), kind=kLoop, calls=%fused_computation.119 | loop fusion | flops 9175040 | bytes 11534336 | tf_op jit(solution)/shard_map/stack | solution.py:282
  236.1 2.4 copy.60
  (138 shorter events, 63.2 us)
Async XLA Ops:
  0.6 15.0 %copy-start.6 = (f32[3]{0:T(128)S(1)}, f32[3]{0:T(128)}, u32[]{:S(2)}) copy-start(f32[3]{0:T(128)} %param.3) | copy-start | bytes 40
  2.5 15.8 %collective-permute-start = (f32[16,3,1024]{2,0,1:T(8,128)S(1)}, f32[16,3,1024]{2,0,1:T(8,128)S(1)}, u32[]{:S(2)}, u32[]{:S(2)}) collective-permute-start(f32[16,3,1024]{2,0,1:T(8,128)S(1)} %get-tuple-element.112), channel_id=1, source_target_pairs={{0,1},{1,2},{2,3},{3,4},{4,5},{5,6},{6,7},{8,9},{9,10},{10,11},{11... | collective-permute-start | bytes 589832 | tf_op jit(solution)/shard_map/ppermute | solution.py:23
  6.1 12.3 %collective-permute-start.3 = (f32[16,3,1024]{2,0,1:T(8,128)S(1)}, f32[16,3,1024]{2,0,1:T(8,128)S(1)}, u32[]{:S(2)}, u32[]{:S(2)}) collective-permute-start(f32[16,3,1024]{2,0,1:T(8,128)S(1)} %get-tuple-element.113), channel_id=1, source_target_pairs={{1,0},{2,1},{3,2},{4,3},{5,4},{6,5},{7,6},{9,8},{10,9},{11,10},{12... | collective-permute-start | bytes 589832 | tf_op jit(solution)/shard_map/ppermute | solution.py:24
  7.5 10.9 %collective-permute-start.1 = (f32[3,16,1024]{2,0,1:T(4,128)S(1)}, f32[3,16,1024]{2,0,1:T(4,128)S(1)}, u32[]{:S(2)}, u32[]{:S(2)}) collective-permute-start(f32[3,16,1024]{2,0,1:T(4,128)S(1)} %get-tuple-element.110), channel_id=1, source_target_pairs={{0,8},{8,16},{16,24},{24,32},{32,40},{40,48},{48,56},{56,64},{64,7... | collective-permute-start | bytes 589832 | tf_op jit(solution)/shard_map/ppermute | solution.py:23
  13.5 10.8 %collective-permute-start.2 = (f32[3,16,1024]{2,0,1:T(4,128)S(1)}, f32[3,16,1024]{2,0,1:T(4,128)S(1)}, u32[]{:S(2)}, u32[]{:S(2)}) collective-permute-start(f32[3,16,1024]{2,0,1:T(4,128)S(1)} %get-tuple-element.111), channel_id=1, source_target_pairs={{8,0},{16,8},{24,16},{32,24},{40,32},{48,40},{56,48},{64,56},{72,6... | collective-permute-start | bytes 589832 | tf_op jit(solution)/shard_map/ppermute | solution.py:24
  32.4 1.4 copy-start.1
  32.4 1.7 copy-start.3
  49.1 8.1 %collective-permute-start.4 = (f32[16,3,1024]{2,0,1:T(8,128)S(1)}, f32[16,3,1024]{2,0,1:T(8,128)S(1)}, u32[]{:S(2)}, u32[]{:S(2)}) collective-permute-start(f32[16,3,1024]{2,0,1:T(8,128)S(1)} %get-tuple-element.108), channel_id=1, source_target_pairs={{0,1},{1,2},{2,3},{3,4},{4,5},{5,6},{6,7},{8,9},{9,10},{10,11},{11... | collective-permute-start | bytes 589832 | tf_op jit(solution)/shard_map/ppermute | solution.py:23
  51.2 7.8 %collective-permute-start.7 = (f32[16,3,1024]{2,0,1:T(8,128)S(1)}, f32[16,3,1024]{2,0,1:T(8,128)S(1)}, u32[]{:S(2)}, u32[]{:S(2)}) collective-permute-start(f32[16,3,1024]{2,0,1:T(8,128)S(1)} %get-tuple-element.109), channel_id=1, source_target_pairs={{1,0},{2,1},{3,2},{4,3},{5,4},{6,5},{7,6},{9,8},{10,9},{11,10},{12... | collective-permute-start | bytes 589832 | tf_op jit(solution)/shard_map/ppermute | solution.py:24
  52.5 12.4 %collective-permute-start.5 = (f32[3,16,1024]{2,0,1:T(4,128)S(1)}, f32[3,16,1024]{2,0,1:T(4,128)S(1)}, u32[]{:S(2)}, u32[]{:S(2)}) collective-permute-start(f32[3,16,1024]{2,0,1:T(4,128)S(1)} %get-tuple-element.106), channel_id=1, source_target_pairs={{0,8},{8,16},{16,24},{24,32},{32,40},{40,48},{48,56},{56,64},{64,7... | collective-permute-start | bytes 589832 | tf_op jit(solution)/shard_map/ppermute | solution.py:23
  55.1 12.7 %collective-permute-start.6 = (f32[3,16,1024]{2,0,1:T(4,128)S(1)}, f32[3,16,1024]{2,0,1:T(4,128)S(1)}, u32[]{:S(2)}, u32[]{:S(2)}) collective-permute-start(f32[3,16,1024]{2,0,1:T(4,128)S(1)} %get-tuple-element.107), channel_id=1, source_target_pairs={{8,0},{16,8},{24,16},{32,24},{40,32},{48,40},{56,48},{64,56},{72,6... | collective-permute-start | bytes 589832 | tf_op jit(solution)/shard_map/ppermute | solution.py:24
  79.2 2.2 copy-start.2
  79.2 2.4 %copy-start.4 = (f32[16,16,1024]{2,1,0:T(8,128)S(1)}, f32[16,16,1024]{2,1,0:T(8,128)}, u32[]{:S(2)}) copy-start(f32[16,16,1024]{2,1,0:T(8,128)} %param.2) | copy-start | bytes 3145732
  96.7 7.8 %collective-permute-start.8 = (f32[16,3,1024]{2,0,1:T(8,128)S(1)}, f32[16,3,1024]{2,0,1:T(8,128)S(1)}, u32[]{:S(2)}, u32[]{:S(2)}) collective-permute-start(f32[16,3,1024]{2,0,1:T(8,128)S(1)} %get-tuple-element.104), channel_id=1, source_target_pairs={{0,1},{1,2},{2,3},{3,4},{4,5},{5,6},{6,7},{8,9},{9,10},{10,11},{11... | collective-permute-start | bytes 589832 | tf_op jit(solution)/shard_map/ppermute | solution.py:23
  98.0 8.9 %collective-permute-start.11 = (f32[16,3,1024]{2,0,1:T(8,128)S(1)}, f32[16,3,1024]{2,0,1:T(8,128)S(1)}, u32[]{:S(2)}, u32[]{:S(2)}) collective-permute-start(f32[16,3,1024]{2,0,1:T(8,128)S(1)} %get-tuple-element.105), channel_id=1, source_target_pairs={{1,0},{2,1},{3,2},{4,3},{5,4},{6,5},{7,6},{9,8},{10,9},{11,10},{12... | collective-permute-start | bytes 589832 | tf_op jit(solution)/shard_map/ppermute | solution.py:24
  99.3 13.3 %collective-permute-start.9 = (f32[3,16,1024]{2,0,1:T(4,128)S(1)}, f32[3,16,1024]{2,0,1:T(4,128)S(1)}, u32[]{:S(2)}, u32[]{:S(2)}) collective-permute-start(f32[3,16,1024]{2,0,1:T(4,128)S(1)} %get-tuple-element.102), channel_id=1, source_target_pairs={{0,8},{8,16},{16,24},{24,32},{32,40},{40,48},{48,56},{56,64},{64,7... | collective-permute-start | bytes 589832 | tf_op jit(solution)/shard_map/ppermute | solution.py:23
  102.3 12.1 %collective-permute-start.10 = (f32[3,16,1024]{2,0,1:T(4,128)S(1)}, f32[3,16,1024]{2,0,1:T(4,128)S(1)}, u32[]{:S(2)}, u32[]{:S(2)}) collective-permute-start(f32[3,16,1024]{2,0,1:T(4,128)S(1)} %get-tuple-element.103), channel_id=1, source_target_pairs={{8,0},{16,8},{24,16},{32,24},{40,32},{48,40},{56,48},{64,56},{72,6... | collective-permute-start | bytes 589832 | tf_op jit(solution)/shard_map/ppermute | solution.py:24
  125.7 2.2 copy-start
  125.7 2.4 %copy-start.5 = (f32[16,16,1024]{2,1,0:T(8,128)S(1)}, f32[16,16,1024]{2,1,0:T(8,128)}, u32[]{:S(2)}) copy-start(f32[16,16,1024]{2,1,0:T(8,128)} %param.2) | copy-start | bytes 3145732
  143.2 8.6 %collective-permute-start.13 = (f32[1,16,1024]{2,0,1:T(1,128)S(1)}, f32[1,16,1024]{2,0,1:T(1,128)S(1)}, u32[]{:S(2)}, u32[]{:S(2)}) collective-permute-start(f32[1,16,1024]{2,0,1:T(1,128)S(1)} %get-tuple-element.98), channel_id=1, source_target_pairs={{0,8},{8,16},{16,24},{24,32},{32,40},{40,48},{48,56},{56,64},{64,7... | collective-permute-start | bytes 196616 | tf_op jit(solution)/shard_map/ppermute | solution.py:23
  147.3 7.7 %collective-permute-start.14 = (f32[1,16,1024]{2,0,1:T(1,128)S(1)}, f32[1,16,1024]{2,0,1:T(1,128)S(1)}, u32[]{:S(2)}, u32[]{:S(2)}) collective-permute-start(f32[1,16,1024]{2,0,1:T(1,128)S(1)} %get-tuple-element.99), channel_id=1, source_target_pairs={{8,0},{16,8},{24,16},{32,24},{40,32},{48,40},{56,48},{64,56},{72,6... | collective-permute-start | bytes 196616 | tf_op jit(solution)/shard_map/ppermute | solution.py:24
  149.2 5.8 %collective-permute-start.12 = (f32[16,1,1024]{2,0,1:T(8,128)S(1)}, f32[16,1,1024]{2,0,1:T(8,128)S(1)}, u32[]{:S(2)}, u32[]{:S(2)}) collective-permute-start(f32[16,1,1024]{2,0,1:T(8,128)S(1)} %get-tuple-element.100), channel_id=1, source_target_pairs={{0,1},{1,2},{2,3},{3,4},{4,5},{5,6},{6,7},{8,9},{9,10},{10,11},{11... | collective-permute-start | bytes 196616 | tf_op jit(solution)/shard_map/ppermute | solution.py:23
  150.5 6.1 %collective-permute-start.15 = (f32[16,1,1024]{2,0,1:T(8,128)S(1)}, f32[16,1,1024]{2,0,1:T(8,128)S(1)}, u32[]{:S(2)}, u32[]{:S(2)}) collective-permute-start(f32[16,1,1024]{2,0,1:T(8,128)S(1)} %get-tuple-element.101), channel_id=1, source_target_pairs={{1,0},{2,1},{3,2},{4,3},{5,4},{6,5},{7,6},{9,8},{10,9},{11,10},{12... | collective-permute-start | bytes 196616 | tf_op jit(solution)/shard_map/ppermute | solution.py:24
  175.0 10.4 %all-to-all-start.1 = ((f32[8,8,16,128]{3,1,2,0:T(8,128)}), f32[8,8,16,128]{3,1,2,0:T(8,128)S(1)}, u32[]{:S(2)}, u32[]{:S(2)}) async-start(f32[8,8,16,128]{3,1,2,0:T(8,128)} %get-tuple-element.96), calls=%async_computation.1 | async-start | bytes 1048576 | tf_op jit(solution)/shard_map/all_to_all | solution.py:57
  185.7 11.4 %collective-permute-start.16 = (f32[1,128,128]{1,2,0:T(8,128)S(1)}, f32[1,128,128]{1,2,0:T(8,128)S(1)}, u32[]{:S(2)}, u32[]{:S(2)}) collective-permute-start(f32[1,128,128]{1,2,0:T(8,128)S(1)} %copy.51), channel_id=1, source_target_pairs={{8,0},{16,8},{24,16},{32,24},{40,32},{48,40},{56,48},{64,56},{72,6... | collective-permute-start | bytes 196616 | tf_op jit(solution)/shard_map/ppermute | solution.py:64
  197.5 4.5 %collective-permute-start.17 = (f32[17,129,1]{1,2,0:T(1,128)S(1)}, f32[17,129,1]{1,2,0:T(1,128)S(1)}, u32[]{:S(2)}, u32[]{:S(2)}) collective-permute-start(f32[17,129,1]{1,2,0:T(1,128)S(1)} %slice.738), channel_id=1, source_target_pairs={{1,0},{2,1},{3,2},{4,3},{5,4},{6,5},{7,6},{9,8},{10,9},{11,10},{12... | collective-permute-start | bytes 26324 | tf_op jit(solution)/shard_map/ppermute | solution.py:64
where the time goes:
time: 240 us; the launch traced here: 239 us
  other arithmetic  102 us (42%)
  starting transfers between devices  49.5 us (21%)
  waiting for transfers between devices  42.6 us (18%)
  local copies, waits for them, and re-layouts  28.7 us (12%)
  blocking collectives  12.4 us (5%)
  between operations  3.38 us (1%)
    ppermute x8, starting transfers between devices, padded_2(): lax.ppermute(last, axis, up)  24 us
    another operation x3, other arithmetic, contour(): return jnp.stack([solve_x, solve_y, solve_z])  22.5 us
    ppermute x8, waiting for transfers between devices, padded_2(): lax.ppermute(leading, axis, [(b, a) for a, b in up])  19.7 us
    add x1, other arithmetic, shards(): 0.75 * level_set  15 us
    add x1, other arithmetic, shards(): 1.0 / 3.0 * level_set  15 us
    add x1, other arithmetic, shards(): phi_one = level_set + advect_rate(widened(level_set, 3), velocity)  14.9 us
    ppermute x8, starting transfers between devices, padded_2(): lax.ppermute(leading, axis, [(b, a) for a, b in up])  13.3 us
    all_to_all x1, blocking collectives, several_exchanges(): lax.all_to_all(share, axis, split_axis=0, concat_axis=0, tiled=True)  12.4 us
  transfers between devices with their start and end apart: 19, of which 12 were waited for; matrix products, arithmetic and copies ran while one was open for 2% of the time, Pallas kernels for 0%

commit v1 on v0

v1 whole, which is shorter than its diff:
```python
import jax
import jax.numpy as jnp
from jax import lax
from jax.experimental import pallas as pl
from jax.experimental.pallas import tpu as pltpu
from jax.sharding import PartitionSpec as P

weno_eps = 1e-06
sharpness = 4.0
crossing_bias = 0.05
mass_prior = 0.05
tikhonov = 0.25
pseudo_step = 0.5
gradient_eps = 1e-06

LOW, HIGH = 10, 11
SHIFT, SLOT = 13, 152
BASE, ROWS, FIRST, SPAN, STEP = 15, 160, 8, 144, 48
VMEM = pl.BlockSpec(memory_space=pltpu.VMEM)
SMEM = pl.BlockSpec(memory_space=pltpu.SMEM)
PARAMS = pltpu.CompilerParams(vmem_limit_bytes=60 * 1024 * 1024)


def pack_kernel(x_ref, out_ref, tall):
    halves, lanes = out_ref.shape[1], out_ref.shape[3]
    layers = x_ref.shape[1]
    for h in range(halves):
        for b in range(layers // lanes):
            tall[h, 16 + b * lanes : 16 + (b + 1) * lanes, :] = x_ref[
                h * lanes : (h + 1) * lanes, b * lanes : (b + 1) * lanes
            ].T
        tall[h, 0:16, :] = jnp.broadcast_to(tall[h, 16:17, :], (16, lanes))
        tall[h, 16 + layers : 32 + layers, :] = jnp.broadcast_to(
            tall[h, 15 + layers : 16 + layers, :], (16, lanes)
        )
    count = out_ref.shape[0]
    for d in range(count):
        start = 16 + d * (layers // count) - SHIFT
        for h in range(halves):
            out_ref[d, h, :, :] = tall[h, start : start + SLOT, :]


def regroup_kernel(in_ref, mid_ref, up_ref, down_ref):
    count, halves, _, lanes = in_ref.shape
    group = lanes // count
    index = lax.broadcasted_iota(jnp.int32, (8, lanes), 1) // group
    rows = mid_ref.shape[0]
    for h in range(halves):

        for t in range(SLOT // 8):
            at = slice(t * 8, t * 8 + 8)
            v = [in_ref[s, h, at, :] for s in range(count)]
            k = count // 2
            while k:
                low_part = (index & k) == 0
                for i in range(count):
                    if i & k:
                        continue
                    a, b = v[i], v[i | k]
                    v[i] = jnp.where(low_part, a, pltpu.roll(b, k * group, 1))
                    v[i | k] = jnp.where(low_part, pltpu.roll(a, lanes - k * group, 1), b)
                k //= 2
            for i in range(count):
                x = h * count + i
                mid_ref[x, at, :] = v[i]
                if x >= rows - LOW:
                    up_ref[x - (rows - LOW), at, :] = v[i]
                if x < HIGH:
                    down_ref[x, at, :] = v[i]


def one_sided(pm2, pm1, p0, pp1, pp2, positive):
    p1 = jnp.where(positive, pm2, pp2)
    p2 = jnp.where(positive, pm1, pp1)
    p4 = jnp.where(positive, pp1, pm1)
    r1 = p2 - p1
    r2 = p0 - p2
    r3 = p4 - p0
    t1 = r2 - r1
    t2 = r3 - r2
    twice_2 = p2 + p2
    y1 = twice_2 + r1
    y2 = twice_2 + r2
    y3 = (p0 + p0) - r3
    k = 13.0 / 3.0
    s1 = (k * r1) * r1 + (y1 * y1 + 4.0 * weno_eps)
    s2 = (k * r2) * r2 + (y2 * y2 + 4.0 * weno_eps)
    s3 = (k * r3) * r3 + (y3 * y3 + 4.0 * weno_eps)
    m1 = s2 * s3
    m2 = s1 * s3
    m3 = s1 * s2
    g1 = m1 * m1
    g2 = (6.0 * m2) * m2
    g3 = (3.0 * m3) * m3
    return r2 + (g1 * (t1 + t1) + g3 * t2) / ((g1 + g3) + g2)


def stage(src, base, dst, coef_refs, scale_ref, lo, count, parts):
    keep, mix = parts
    lanes = src.shape[2]
    lane = lax.broadcasted_iota(jnp.int32, (STEP, lanes), 1)

    def along_lanes(f):
        fp = jnp.where(lane == lanes - 1, f, pltpu.roll(f, lanes - 1, 1))
        fm = jnp.where(lane == 0, f, pltpu.roll(f, 1, 1))
        return (fp - f) - (f - fm), fp - fm

    for start in range(FIRST, FIRST + SPAN, STEP):
        coefs = [ref[start : start + STEP, :] for ref in coef_refs]

        def at(x, shift=0, start=start):
            return src[x, start + shift : start + shift + STEP, :]

        def body(i, carry, start=start, coefs=coefs, at=at):
            x = lo + i
            pm2, pm1, p0, pp1, last, q0, across = carry
            f = at(x)
            following = along_lanes(at(x + 1))
            qm1 = jnp.where(lane < 1, 0.0, pltpu.roll(q0, 1, 1))
            qm2 = jnp.where(lane < 2, 0.0, pltpu.roll(q0, 2, 1))
            qp1 = jnp.where(lane > lanes - 2, 0.0, pltpu.roll(q0, lanes - 1, 1))
            qp2 = jnp.where(lane > lanes - 3, 0.0, pltpu.roll(q0, lanes - 2, 1))
            ahead, near = at(x + 3), at(x + 2)
            step = ahead - near
            pp2 = step - last
            speed = scale_ref[0, x] * coefs[0]
            total = speed * (at(x + 1) - at(x - 1))
            damp = jnp.abs(speed) * one_sided(pm2, pm1, p0, pp1, pp2, speed > 0)
            z = [at(x, shift) for shift in (-3, -2, -1)] + [f]
            z = z + [at(x, shift) for shift in (1, 2, 3)]
            d = [z[n + 1] - z[n] for n in range(6)]
            q = [d[n + 1] - d[n] for n in range(5)]
            speed = scale_ref[2, x] * coefs[2]
            total = total + speed * (z[4] - z[2])
            damp = damp + jnp.abs(speed) * one_sided(*q, speed > 0)
            speed = scale_ref[1, x] * coefs[1]
            total = total + speed * across
            damp = damp + jnp.abs(speed) * one_sided(qm2, qm1, q0, qp1, qp2, speed > 0)
            moved = f - (total - (1.0 / 3.0) * damp)
            if base is not None:
                moved = keep * base[x, start : start + STEP, :] + mix * moved
            dst[x, start : start + STEP, :] = moved
            return (pm1, p0, pp1, pp2, step, *following)

        f = [at(lo + n) for n in range(-3, 3)]
        d = [f[n + 1] - f[n] for n in range(5)]
        p = [d[n + 1] - d[n] for n in range(4)]
        lax.fori_loop(0, count, body, (p[0], p[1], p[2], p[3], d[4], *along_lanes(at(lo))))


def clamp_planes(ref, first, last, lo, hi, begin, end):
    @pl.when(first)
    def _():
        def fill(i, carry):
            ref[lo + i] = ref[begin]
            return carry

        lax.fori_loop(0, begin - lo, fill, 0)

    @pl.when(last)
    def _():
        def fill(i, carry):
            ref[end + i] = ref[end - 1]
            return carry

        lax.fori_loop(0, hi - end, fill, 0)


def clamp_rows(ref, first, last, lo, hi, depth):
    @pl.when(first)
    def _():
        def fill(i, carry):
            x = lo + i
            ref[x, FIRST:BASE, :] = jnp.broadcast_to(
                ref[x, BASE : BASE + 1, :], (BASE - FIRST, ref.shape[2])
            )
            return carry

        lax.fori_loop(0, hi - lo, fill, 0)

    @pl.when(last)
    def _():
        def fill(i, carry):
            x = lo + i
            top = BASE + depth
            ref[x, top : FIRST + SPAN, :] = jnp.broadcast_to(
                ref[x, top - 1 : top, :], (FIRST + SPAN - top, ref.shape[2])
            )
            return carry

        lax.fori_loop(0, hi - lo, fill, 0)


def one_side(positive, behind, forward):
    growing = jnp.maximum(jnp.maximum(behind, 0.0) ** 2, jnp.minimum(forward, 0.0) ** 2)
    falling = jnp.maximum(jnp.minimum(behind, 0.0) ** 2, jnp.maximum(forward, 0.0) ** 2)
    return jnp.where(positive, growing, falling)


def sweep(src, dst, lo, count):
    lanes = src.shape[2]
    lane = lax.broadcasted_iota(jnp.int32, (STEP, lanes), 1)

    def body(i, carry):
        x = lo + i
        for start in range(FIRST, FIRST + SPAN, STEP):

            def at(x, shift=0, start=start):
                return src[x, start + shift : start + shift + STEP, :]

            s = at(x)
            positive = s > 0
            sp = jnp.where(lane == lanes - 1, s, pltpu.roll(s, lanes - 1, 1))
            sm = jnp.where(lane == 0, s, pltpu.roll(s, 1, 1))
            total = one_side(positive, s - at(x - 1), at(x + 1) - s)
            total = total + one_side(positive, s - at(x, -1), at(x, 1) - s)
            total = total + one_side(positive, s - sm, sp - s)
            size = jnp.sqrt(total + gradient_eps)
            sign = s / jnp.sqrt(s * s + 1.0)
            dst[x, start : start + STEP, :] = s - pseudo_step * sign * (size - 1.0)
        return carry

    lax.fori_loop(0, count, body, 0)


def step_kernel(
    place_ref, scale_ref, u_ref, v_ref, w_ref, mid_ref, low_ref, high_ref,
    slots_ref, lower_ref, upper_ref, f0, f1, f2,
):
    own, depth = mid_ref.shape[0], lower_ref.shape[2]
    begin, end = LOW, LOW + own
    first_x = place_ref[0] == 0
    last_x = place_ref[0] == place_ref[2] - 1
    first_z = place_ref[1] == 0
    last_z = place_ref[1] == place_ref[3] - 1
    shift = BASE - SHIFT
    for ref, begin_at in ((low_ref, 0), (mid_ref, begin), (high_ref, end)):

        def move(i, carry, ref=ref, begin_at=begin_at):
            f0[begin_at + i, shift : shift + SLOT, :] = ref[i]
            return carry

        lax.fori_loop(0, ref.shape[0], move, 0)
    clamp_planes(f0, first_x, last_x, 0, end + HIGH, begin, end)
    coefs = (u_ref, v_ref, w_ref)
    plan = ((f0, None, f1, 3, None), (f1, f0, f2, 6, (0.75, 0.25)), (f2, f0, f1, 9, (1.0 / 3.0, 2.0 / 3.0)))
    total = end + HIGH
    for src, base, dst, inset, parts in plan:
        stage(src, base, dst, coefs, scale_ref, inset, total - 2 * inset, parts or (0.0, 1.0))
        clamp_planes(dst, first_x, last_x, inset, total - inset, begin, end)
        clamp_rows(dst, first_z, last_z, inset, total - inset, depth)
    sweep(f1, f0, begin, own + 1)
    clamp_planes(f0, jnp.bool_(False), last_x, begin, end + 1, begin, end)
    clamp_rows(f0, jnp.bool_(False), last_z, begin, end + 1, depth)
    count = slots_ref.shape[0]
    piece = depth // count

    def turn(i, carry):
        lower = f0[begin + i, BASE : BASE + depth, :].T
        upper = f0[begin + i, BASE + 1 : BASE + 1 + depth, :].T
        for ref, value in ((lower_ref, lower), (upper_ref, upper)):
            ref[i, 0:depth, :] = value
            ref[i, depth : depth + 8, :] = jnp.broadcast_to(value[depth - 1 : depth], (8, depth))

        @pl.when(i < own)
        def _():
            for d in range(count):
                slots_ref[d, i] = lower[d * piece : (d + 1) * piece]

        return carry

    lax.fori_loop(0, own + 1, turn, 0)


def edge_terms(a, b):
    weight = 1.0 / (1.0 + jnp.exp2((sharpness * 1.4426950408889634) * (a * b)))
    low = a * a + crossing_bias
    return weight, low / (low + (b * b + crossing_bias))


def contour_kernel(lower_ref, upper_ref, out_ref, wz, tz, wy, ty, wx, tx):
    planes, _, lanes = lower_ref.shape
    depth = lanes
    sides = (lower_ref, upper_ref)

    def edges(x, carry):
        for start in range(0, depth + 8, 8):
            at = slice(start, start + 8)
            wz[x, at, :], tz[x, at, :] = edge_terms(lower_ref[x, at, :], upper_ref[x, at, :])
            for n, ref in enumerate(sides):
                if start < depth:
                    here, there = ref[x, at, :], ref[x, start + 1 : start + 9, :]
                    wy[n, x, at, :], ty[n, x, at, :] = edge_terms(here, there)

                @pl.when(x < planes - 1)
                def _(n=n, ref=ref, at=at, x=x):
                    wx[n, x, at, :], tx[n, x, at, :] = edge_terms(ref[x, at, :], ref[x + 1, at, :])

        return carry

    lax.fori_loop(0, planes, edges, 0)

    def cubes(x, carry):
        for start in range(0, depth, 8):

            def rows(bit, start=start):
                return slice(start + bit, start + bit + 8)

            f = {}
            for bx in (0, 1):
                for by in (0, 1):
                    for bz in (0, 1):
                        f[bx, by, bz] = sides[bz][x + bx, rows(by), :]
            diff = {}
            for d in range(3):
                for key in sorted(f):
                    if key[d] == 0:
                        diff[d, key] = f[set_bit(key, d, 1)] - f[key]
            total = None
            mass = [None] * 3
            moment = {}
            target = [None] * 3

            def add(old, new):
                return new if old is None else old + new

            for d in range(3):
                for key in sorted(f):
                    if key[d] != 0:
                        continue
                    bx, by, bz = key
                    if d == 0:
                        weight, part = wx[bz, x, rows(by), :], tx[bz, x, rows(by), :]
                    elif d == 1:
                        weight, part = wy[bz, x + bx, rows(0), :], ty[bz, x + bx, rows(0), :]
                    else:
                        weight, part = wz[x + bx, rows(by), :], tz[x + bx, rows(by), :]
                    normal = [None] * 3
                    normal[d] = diff[d, key]
                    for a in range(3):
                        if a != d:
                            low = diff[a, set_bit(key, a, 0)]
                            high = diff[a, set_bit(set_bit(key, a, 0), d, 1)]
                            normal[a] = low + part * (high - low)
                    projection = normal[d] * part
                    for a in range(3):
                        if a != d and key[a] == 1:
                            projection = projection + normal[a]
                            mass[a] = add(mass[a], weight)
                    total = add(total, weight)
                    mass[d] = add(mass[d], weight * part)
                    scaled = [weight * n for n in normal]
                    for i in range(3):
                        for j in range(i, 3):
                            moment[i, j] = add(moment.get((i, j)), scaled[i] * normal[j])
                        target[i] = add(target[i], scaled[i] * projection)
            inverse = tikhonov / (total + mass_prior)
            right = [target[i] + (mass[i] + 0.5 * mass_prior) * inverse for i in range(3)]
            for i in range(3):
                moment[i, i] = moment[i, i] + tikhonov
            s = moment
            c00 = s[1, 1] * s[2, 2] - s[1, 2] * s[1, 2]
            c01 = s[0, 2] * s[1, 2] - s[0, 1] * s[2, 2]
            c02 = s[0, 1] * s[1, 2] - s[0, 2] * s[1, 1]
            c11 = s[0, 0] * s[2, 2] - s[0, 2] * s[0, 2]
            c12 = s[0, 1] * s[0, 2] - s[0, 0] * s[1, 2]
            c22 = s[0, 0] * s[1, 1] - s[0, 1] * s[0, 1]
            over = 1.0 / (s[0, 0] * c00 + s[0, 1] * c01 + s[0, 2] * c02)
            out_ref[0, x, rows(0), :] = (c00 * right[0] + c01 * right[1] + c02 * right[2]) * over
            out_ref[1, x, rows(0), :] = (c01 * right[0] + c11 * right[1] + c12 * right[2]) * over
            out_ref[2, x, rows(0), :] = (c02 * right[0] + c12 * right[1] + c22 * right[2]) * over
        return carry

    lax.fori_loop(0, planes - 1, cubes, 0)


def set_bit(key, d, value):
    listed = list(key)
    listed[d] = value
    return tuple(listed)


def speeds(flow_amplitude, x_start, z_start, own, depth, total_x, total_y, total_z):
    def cells(start, count, total):
        return ((start + jnp.arange(count, dtype=jnp.int32)).astype(jnp.float32) + 0.5) / total

    x = cells(x_start - LOW, LOW + own + HIGH, total_x)
    y = cells(0, total_y, total_y)
    z = cells(z_start - BASE, ROWS, total_z)
    half_x, full_x = jnp.sin(jnp.pi * x) ** 2, jnp.sin(2.0 * jnp.pi * x)
    half_y, full_y = jnp.sin(jnp.pi * y) ** 2, jnp.sin(2.0 * jnp.pi * y)
    half_z, full_z = jnp.sin(jnp.pi * z) ** 2, jnp.sin(2.0 * jnp.pi * z)
    scale = jnp.stack(
        [
            flow_amplitude[0] * half_x,
            -0.5 * flow_amplitude[1] * full_x,
            -0.5 * flow_amplitude[2] * full_x,
        ]
    )
    u = full_z[:, None] * full_y[None, :]
    v = full_z[:, None] * half_y[None, :]
    w = half_z[:, None] * full_y[None, :]
    return scale, u, v, w


def shards(level_set, flow_amplitude):
    own, cols, layers = level_set.shape
    count_x, count_z = lax.axis_size("px"), lax.axis_size("py")
    at_x, at_z = lax.axis_index("px"), lax.axis_index("py")
    depth, wide = layers // count_z, cols * count_z
    lanes = 128
    halves = own * cols // lanes
    f32 = jnp.float32
    slots = pl.pallas_call(
        pack_kernel,
        out_shape=jax.ShapeDtypeStruct((count_z, halves, SLOT, lanes), f32),
        in_specs=[VMEM],
        out_specs=VMEM,
        scratch_shapes=[pltpu.VMEM((halves, layers + 32, lanes), f32)],
        compiler_params=PARAMS,
        name="pack",
    )(level_set.reshape(own * cols, layers))
    slots = lax.all_to_all(slots, "py", split_axis=0, concat_axis=0, tiled=True)
    mid, up, down = pl.pallas_call(
        regroup_kernel,
        out_shape=[jax.ShapeDtypeStruct((n, SLOT, wide), f32) for n in (own, LOW, HIGH)],
        in_specs=[VMEM],
        out_specs=[VMEM] * 3,
        compiler_params=PARAMS,
        name="regroup",
    )(slots)
    ring = [(i, (i + 1) % count_x) for i in range(count_x)]
    low = lax.ppermute(up, "px", ring)
    high = lax.ppermute(down, "px", [(b, a) for a, b in ring])
    scale, u, v, w = speeds(
        flow_amplitude, at_x * own, at_z * depth, own, depth, own * count_x, wide, layers
    )
    place = jnp.stack([at_x, at_z, jnp.int32(count_x), jnp.int32(count_z)]).astype(jnp.int32)
    planes = LOW + own + HIGH
    turned, lower, upper = pl.pallas_call(
        step_kernel,
        out_shape=[
            jax.ShapeDtypeStruct((count_z, own, cols, depth), f32),
            jax.ShapeDtypeStruct((own + 1, wide + 8, depth), f32),
            jax.ShapeDtypeStruct((own + 1, wide + 8, depth), f32),
        ],
        in_specs=[SMEM, SMEM] + [VMEM] * 6,
        out_specs=[VMEM] * 3,
        scratch_shapes=[pltpu.VMEM((planes, ROWS, wide), f32)] * 3,
        compiler_params=PARAMS,
        name="advance",
    )(place, scale, u, v, w, mid, low, high)
    back = lax.all_to_all(turned, "py", split_axis=0, concat_axis=0, tiled=True)
    phi_next = jnp.moveaxis(back, 0, 2).reshape(own, cols, layers)
    vertices = pl.pallas_call(
        contour_kernel,
        out_shape=jax.ShapeDtypeStruct((3, own, wide, depth), f32),
        in_specs=[VMEM] * 2,
        out_specs=VMEM,
        scratch_shapes=[pltpu.VMEM((own + 1, wide + 8, depth), f32)] * 2
        + [pltpu.VMEM((2, own + 1, wide, depth), f32)] * 2
        + [pltpu.VMEM((2, own, wide + 8, depth), f32)] * 2,
        compiler_params=PARAMS,
        name="contour",
    )(lower, upper)
    return (phi_next, vertices)


def solution(mesh):
    in_specs = (P("px", "py", None), P())
    out_specs = (P("px", "py", None), P(None, "px", None, "py"))
    return jax.shard_map(shards, mesh=mesh, in_specs=in_specs, out_specs=out_specs, check_vma=False)
```

time: 240 us -> 148 us (0.62)
  other arithmetic: 102 us -> 2.81 us
  Pallas kernels: 0 us -> 92.3 us
  starting transfers between devices: 49.5 us -> 13.9 us
  local copies, waits for them, and re-layouts: 28.7 us -> 3.62 us
  blocking collectives: 12.4 us -> 0 us
  waiting for transfers between devices: 42.6 us -> 32.6 us
    pallas_call x0 -> x4, Pallas kernels: none -> 92.3 us  [the longest x1 50.4 us: shards(): pl.pallas_call(step_kernel, out_shape=[jax.ShapeDtypeStruct((count_z, own...]
    add x3 -> x0, other arithmetic: 44.8 us -> none  [the longest x1 15 us: shards(): 0.75 * level_set]
    ppermute x18 -> x2, starting transfers between devices: 46 us -> 4.83 us  [the longest x1 3.26 us: shards(): low = lax.ppermute(up, 'px', ring)]
    another operation x3 -> x2, other arithmetic: 22.5 us -> 1.21 us  [the longest x1 0.65 us: shards(): jnp.stack([at_x, at_z, jnp.int32(count_x), jnp.int32(count_z)])]
    sub x15 -> x0, other arithmetic: 21.2 us -> none  [the longest x9 9.79 us: upwind_pair(): lax.slice_in_dim(padded, 1, length + 6, axis=dimension)]
    ppermute x18 -> x2, waiting for transfers between devices: 35.7 us -> 16.1 us  [the longest x1 15.5 us: shards(): low = lax.ppermute(up, 'px', ring)]
    all_to_all x1 -> x0, blocking collectives: 12.4 us -> none  [several_exchanges(): lax.all_to_all(share, axis, split_axis=0, concat_axis=0, tiled=True)]
    all_to_all x1 -> x2, waiting for transfers between devices: 6.89 us -> 16.6 us  [the longest x1 16.6 us: shards(): slots = lax.all_to_all(slots, 'py', split_axis=0, concat_axis=0, tiled=True)]
  transfers between devices with their start and end apart: 19 -> 4, of which waited for: 12 -> 3; matrix products, arithmetic and copies ran while one was open for 2% -> 2% of each run, Pallas kernels for 0% -> 21%
where the time goes in v1:
time: 148 us; the launch traced here: 147 us
  Pallas kernels  92.3 us (62%)
  waiting for transfers between devices  32.6 us (22%)
  starting transfers between devices  13.9 us (9%)
  local copies, waits for them, and re-layouts  3.62 us (2%)
  other arithmetic  2.81 us (2%)
  between operations  1.88 us (1%)
    pallas_call x1, Pallas kernels, shards(): pl.pallas_call(step_kernel, out_shape=[jax.ShapeDtypeStruct((count_z, own...  50.4 us
    pallas_call x1, Pallas kernels, shards(): pl.pallas_call(contour_kernel, out_shape=jax.ShapeDtypeStruct((3, own, wi...  31.6 us
    all_to_all x1, waiting for transfers between devices, shards(): slots = lax.all_to_all(slots, 'py', split_axis=0, concat_axis=0, tiled=True)  16.6 us
    ppermute x1, waiting for transfers between devices, shards(): low = lax.ppermute(up, 'px', ring)  15.5 us
    pallas_call x1, Pallas kernels, shards(): pl.pallas_call(regroup_kernel, out_shape=[jax.ShapeDtypeStruct((n, SLOT,...  7.69 us
    all_to_all x1, starting transfers between devices, shards(): slots = lax.all_to_all(slots, 'py', split_axis=0, concat_axis=0, tiled=True)  5.51 us
    all_to_all x1, starting transfers between devices, shards(): back = lax.all_to_all(turned, 'py', split_axis=0, concat_axis=0, tiled=True)  3.56 us
    ppermute x1, starting transfers between devices, shards(): low = lax.ppermute(up, 'px', ring)  3.26 us
  transfers between devices with their start and end apart: 4, of which 3 were waited for; matrix products, arithmetic and copies ran while one was open for 2% of the time, Pallas kernels for 21%

profile of v1, /device:TPU:9, one launch (start us, length us, event | category | flops | bytes accessed | tf_op | source)
XLA Modules:
  0.0 147.2 jit_solution(4586144498195752160)
XLA Ops:
  0.6 2.7 %pack.1 = f32[8,2,152,128]{3,2,1,0:T(8,128)} custom-call(f32[256,1024]{1,0:T(8,128)} %bitcast.12), custom_call_target="tpu_custom_call" | custom-call | tf_op jit(solution)/shard_map/pack/pallas_call | solution.py:414
  3.3 0.0 copy-start.3
  3.3 5.5 %all-to-all-start = ((f32[8,2,152,128]{3,2,1,0:T(8,128)}), f32[8,2,152,128]{3,2,1,0:T(8,128)S(1)}, u32[]{:S(2)}, u32[]{:S(2)}) async-start(f32[8,2,152,128]{3,2,1,0:T(8,128)} %pack.1), calls=%async_computation | async-start | bytes 2490368 | tf_op jit(solution)/shard_map/all_to_all | solution.py:423
  8.9 0.0 copy-done.3
  8.9 0.6 fusion
  10.7 16.6 %all-to-all-done.in_ref = f32[8,2,152,128]{3,2,1,0:T(8,128)S(1)} async-done(((f32[8,2,152,128]{3,2,1,0:T(8,128)}), f32[8,2,152,128]{3,2,1,0:T(8,128)S(1)}, u32[]{:S(2)}, u32[]{:S(2)}) %all-to-all-start) | async-done | bytes 1245216 | tf_op jit(solution)/shard_map/all_to_all | solution.py:423
  27.2 0.0 copy-start
  27.2 1.0 copy-done
  28.3 7.7 %regroup.1 = (f32[16,152,128]{2,1,0:T(8,128)}, f32[10,152,128]{2,1,0:T(8,128)}, f32[11,152,128]{2,1,0:T(8,128)}) custom-call(f32[8,2,152,128]{3,2,1,0:T(8,128)} %copy-done), custom_call_target="tpu_custom_call" | custom-call | tf_op jit(solution)/shard_map/regroup/pallas_call | solution.py:424
  36.0 1.6 %collective-permute-start.1 = (f32[11,152,128]{2,1,0:T(8,128)}, f32[11,152,128]{2,1,0:T(8,128)S(1)}, u32[]{:S(2)}, u32[]{:S(2)}) collective-permute-start(f32[11,152,128]{2,1,0:T(8,128)} %get-tuple-element.10), channel_id=1, source_target_pairs={{8,0},{16,8},{24,16},{32,24},{40,32},{48,40},{56,48},{64,56},{72,6... | collective-permute-start | bytes 2568200 | tf_op jit(solution)/shard_map/ppermute | solution.py:434
  37.6 3.3 %collective-permute-start = (f32[10,152,128]{2,1,0:T(8,128)}, f32[10,152,128]{2,1,0:T(8,128)S(1)}, u32[]{:S(2)}, u32[]{:S(2)}) collective-permute-start(f32[10,152,128]{2,1,0:T(8,128)} %get-tuple-element.9), channel_id=1, source_target_pairs={{0,8},{8,16},{16,24},{24,32},{32,40},{40,48},{48,56},{56,64},{64,7... | collective-permute-start | bytes 2334728 | tf_op jit(solution)/shard_map/ppermute | solution.py:433
  40.8 0.7 pad_add_fusion.place_ref
  41.5 0.1 sine_multiply_fusion.1
  41.5 0.7 multiply_multiply_fusion
  42.2 0.1 sine_multiply_fusion
  42.3 0.6 pad_maximum_fusion.scale_ref
  42.8 0.8 broadcast_multiply_fusion.1
  43.6 15.5 %collective-permute-done.low_ref = f32[10,152,128]{2,1,0:T(8,128)S(1)} collective-permute-done((f32[10,152,128]{2,1,0:T(8,128)}, f32[10,152,128]{2,1,0:T(8,128)S(1)}, u32[]{:S(2)}, u32[]{:S(2)}) %collective-permute-start) | collective-permute-done | bytes 778272 | tf_op jit(solution)/shard_map/ppermute | solution.py:433
  59.1 0.0 copy-start.2
  59.1 0.6 collective-permute-done.1.high_ref
  59.7 0.0 copy-start.1
  59.7 0.3 copy-done.2
  59.9 0.6 copy-done.1
  60.6 50.4 %advance.1 = (f32[8,16,16,128]{3,2,1,0:T(8,128)}, f32[17,136,128]{2,1,0:T(8,128)}, f32[17,136,128]{2,1,0:T(8,128)}) custom-call(s32[4]{0:T(128)} %pad_add_fusion.place_ref, f32[3,37]{1,0:T(4,128)} %pad_maximum_fusion.scale_ref, f32[160,128]{1,0:T(8,128)} %get-tuple-element.15.u_ref, f32[160,128]{1,0:T(8,128)} %get-tuple-element.14.v_ref, ...), custom_call_target="tpu_custom_call" | custom-call | tf_op jit(solution)/shard_map/advance/pallas_call | solution.py:440
  111.0 3.6 %all-to-all-start.1 = ((f32[8,16,16,128]{3,2,1,0:T(8,128)}), f32[8,16,16,128]{3,2,1,0:T(8,128)S(1)}, u32[]{:S(2)}, u32[]{:S(2)}) async-start(f32[8,16,16,128]{3,2,1,0:T(8,128)} %get-tuple-element.11), calls=%async_computation.1 | async-start | bytes 2097152 | tf_op jit(solution)/shard_map/all_to_all | solution.py:453
  114.5 31.6 %contour.1 = f32[3,16,128,128]{3,2,1,0:T(8,128)} custom-call(f32[17,136,128]{2,1,0:T(8,128)} %get-tuple-element.12.lower_ref, f32[17,136,128]{2,1,0:T(8,128)} %get-tuple-element.13.upper_ref), custom_call_target="tpu_custom_call" | custom-call | tf_op jit(solution)/shard_map/contour/pallas_call | solution.py:455
  146.1 0.0 all-to-all-done.1
  146.1 1.1 copy_bitcast_fusion
  (1 shorter events, 0.0 us)
Async XLA Ops:
  3.3 5.5 %copy-start.3 = (f32[3]{0:T(128)S(1)}, f32[3]{0:T(128)}, u32[]{:S(2)}) copy-start(f32[3]{0:T(128)} %param.3) | copy-start | bytes 40
  3.3 23.9 %all-to-all-start = ((f32[8,2,152,128]{3,2,1,0:T(8,128)}), f32[8,2,152,128]{3,2,1,0:T(8,128)S(1)}, u32[]{:S(2)}, u32[]{:S(2)}) async-start(f32[8,2,152,128]{3,2,1,0:T(8,128)} %pack.1), calls=%async_computation | async-start | bytes 2490368 | tf_op jit(solution)/shard_map/all_to_all | solution.py:423
  27.2 1.0 copy-start
  36.0 23.7 %collective-permute-start.1 = (f32[11,152,128]{2,1,0:T(8,128)}, f32[11,152,128]{2,1,0:T(8,128)S(1)}, u32[]{:S(2)}, u32[]{:S(2)}) collective-permute-start(f32[11,152,128]{2,1,0:T(8,128)} %get-tuple-element.10), channel_id=1, source_target_pairs={{8,0},{16,8},{24,16},{32,24},{40,32},{48,40},{56,48},{64,56},{72,6... | collective-permute-start | bytes 2568200 | tf_op jit(solution)/shard_map/ppermute | solution.py:434
  37.6 21.5 %collective-permute-start = (f32[10,152,128]{2,1,0:T(8,128)}, f32[10,152,128]{2,1,0:T(8,128)S(1)}, u32[]{:S(2)}, u32[]{:S(2)}) collective-permute-start(f32[10,152,128]{2,1,0:T(8,128)} %get-tuple-element.9), channel_id=1, source_target_pairs={{0,8},{8,16},{16,24},{24,32},{32,40},{40,48},{48,56},{56,64},{64,7... | collective-permute-start | bytes 2334728 | tf_op jit(solution)/shard_map/ppermute | solution.py:433
  59.1 0.9 copy-start.2
  59.7 0.9 copy-start.1
  111.0 35.1 %all-to-all-start.1 = ((f32[8,16,16,128]{3,2,1,0:T(8,128)}), f32[8,16,16,128]{3,2,1,0:T(8,128)S(1)}, u32[]{:S(2)}, u32[]{:S(2)}) async-start(f32[8,16,16,128]{3,2,1,0:T(8,128)} %get-tuple-element.11), calls=%async_computation.1 | async-start | bytes 2097152 | tf_op jit(solution)/shard_map/all_to_all | solution.py:453

commit v2 on v1

v2 whole, which is shorter than its diff:
```python
import jax
import jax.numpy as jnp
from jax import lax
from jax.experimental import pallas as pl
from jax.experimental.pallas import tpu as pltpu
from jax.sharding import PartitionSpec as P

weno_eps = 1e-06
sharpness = 4.0
crossing_bias = 0.05
mass_prior = 0.05
tikhonov = 0.25
pseudo_step = 0.5
gradient_eps = 1e-06

EDGE = 8
LOW, HIGH = 4, 5
SHIFT, SLOT = 13, 152
BASE, ROWS, FIRST, SPAN, STEP = 15, 160, 8, 144, 48
LATE = ((14, 48), (62, 48), (110, 40))
VMEM = pl.BlockSpec(memory_space=pltpu.VMEM)
SMEM = pl.BlockSpec(memory_space=pltpu.SMEM)
PARAMS = pltpu.CompilerParams(vmem_limit_bytes=24 * 1024 * 1024)
WIDE_PARAMS = pltpu.CompilerParams(vmem_limit_bytes=48 * 1024 * 1024)


def pack_kernel(x_ref, out_ref, tall):
    halves, lanes = out_ref.shape[1], out_ref.shape[3]
    layers = x_ref.shape[1]
    for h in range(halves):
        for b in range(layers // lanes):
            tall[h, 16 + b * lanes : 16 + (b + 1) * lanes, :] = x_ref[
                h * lanes : (h + 1) * lanes, b * lanes : (b + 1) * lanes
            ].T
        tall[h, 0:16, :] = jnp.broadcast_to(tall[h, 16:17, :], (16, lanes))
        tall[h, 16 + layers : 32 + layers, :] = jnp.broadcast_to(
            tall[h, 15 + layers : 16 + layers, :], (16, lanes)
        )
    count = out_ref.shape[0]
    for d in range(count):
        start = 16 + d * (layers // count) - SHIFT
        for h in range(halves):
            out_ref[d, h, :, :] = tall[h, start : start + SLOT, :]


def regroup(read, count, lanes, planes, write):
    group = lanes // count
    index = lax.broadcasted_iota(jnp.int32, (8, lanes), 1) // group
    for t in range(SLOT // 8):
        at = slice(t * 8, t * 8 + 8)
        v = [read(n, at) for n in range(count)]
        k = count // 2
        while k:
            low_part = (index & k) == 0
            for i in range(count):
                if i & k:
                    continue
                a, b = v[i], v[i | k]
                v[i] = jnp.where(low_part, a, pltpu.roll(b, k * group, 1))
                v[i | k] = jnp.where(low_part, pltpu.roll(a, lanes - k * group, 1), b)
            k //= 2
        start = BASE - SHIFT + t * 8
        for i in planes:
            write(i, slice(start, start + 8), v[i])


def one_sided(pm2, pm1, p0, pp1, pp2, positive):
    p1 = jnp.where(positive, pm2, pp2)
    p2 = jnp.where(positive, pm1, pp1)
    p4 = jnp.where(positive, pp1, pm1)
    r2 = p0 - p2
    t1 = r2 - (p2 - p1)
    t2 = (p4 - p0) - r2
    k = 39.0 / 64.0
    eps = 0.75 * weno_eps
    c2 = (k * p2) * p2 + eps
    c0 = (k * p0) * p0 + eps
    y1 = p1 - 1.375 * p2
    y2 = p0 - 0.625 * p2
    y3 = p4 - 1.375 * p0
    s1 = y1 * y1 + c2
    s2 = y2 * y2 + c2
    s3 = y3 * y3 + c0
    g1, g2, g3 = [over * over for over in (1.0 / s1, 1.0 / s2, 1.0 / s3)]
    g3 = 3.0 * g3
    return r2 + (g1 * (t1 + t1) + g3 * t2) / ((g1 + g3) + 6.0 * g2)


def stage(src, base, dst, coef_refs, scale_ref, lo, count, parts, rows=None):
    keep, mix = parts
    lanes = src.shape[2]

    def along_lanes(f):
        lane = lax.broadcasted_iota(jnp.int32, f.shape, 1)
        fp = jnp.where(lane == lanes - 1, f, pltpu.roll(f, lanes - 1, 1))
        fm = jnp.where(lane == 0, f, pltpu.roll(f, 1, 1))
        return (fp - f) - (f - fm), fp - fm

    for start, step_rows in rows or [(n, STEP) for n in range(FIRST, FIRST + SPAN, STEP)]:
        part = slice(start, start + step_rows)
        coefs = [ref[part, :] for ref in coef_refs]
        lane = lax.broadcasted_iota(jnp.int32, (step_rows, lanes), 1)

        def at(x, shift=0, start=start, step_rows=step_rows):
            return src[x, start + shift : start + shift + step_rows, :]

        def body(i, carry, part=part, coefs=coefs, lane=lane, at=at):
            x = lo + i
            pm2, pm1, p0, pp1, last, q0, across = carry
            f = at(x)
            following = along_lanes(at(x + 1))
            qm1 = jnp.where(lane < 1, 0.0, pltpu.roll(q0, 1, 1))
            qm2 = jnp.where(lane < 2, 0.0, pltpu.roll(q0, 2, 1))
            qp1 = jnp.where(lane > lanes - 2, 0.0, pltpu.roll(q0, lanes - 1, 1))
            qp2 = jnp.where(lane > lanes - 3, 0.0, pltpu.roll(q0, lanes - 2, 1))
            ahead, near = at(x + 3), at(x + 2)
            step = ahead - near
            pp2 = step - last
            speed = scale_ref[0, x] * coefs[0]
            total = speed * (at(x + 1) - at(x - 1))
            damp = jnp.abs(speed) * one_sided(pm2, pm1, p0, pp1, pp2, speed > 0)
            z = [at(x, shift) for shift in (-3, -2, -1)] + [f]
            z = z + [at(x, shift) for shift in (1, 2, 3)]
            d = [z[n + 1] - z[n] for n in range(6)]
            q = [d[n + 1] - d[n] for n in range(5)]
            speed = scale_ref[2, x] * coefs[2]
            total = total + speed * (z[4] - z[2])
            damp = damp + jnp.abs(speed) * one_sided(*q, speed > 0)
            speed = scale_ref[1, x] * coefs[1]
            total = total + speed * across
            damp = damp + jnp.abs(speed) * one_sided(qm2, qm1, q0, qp1, qp2, speed > 0)
            moved = f - (total - (1.0 / 3.0) * damp)
            if base is not None:
                moved = keep * base[x, part, :] + mix * moved
            dst[x, part, :] = moved
            return (pm1, p0, pp1, pp2, step, *following)

        f = [at(lo + n) for n in range(-3, 3)]
        d = [f[n + 1] - f[n] for n in range(5)]
        p = [d[n + 1] - d[n] for n in range(4)]
        lax.fori_loop(0, count, body, (p[0], p[1], p[2], p[3], d[4], *along_lanes(at(lo))))


def clamp_planes(ref, first, last, lo, hi, begin, end):
    @pl.when(first)
    def _():
        def fill(i, carry):
            ref[lo + i] = ref[begin]
            return carry

        lax.fori_loop(0, begin - lo, fill, 0)

    @pl.when(last)
    def _():
        def fill(i, carry):
            ref[end + i] = ref[end - 1]
            return carry

        lax.fori_loop(0, hi - end, fill, 0)


def clamp_rows(ref, first, last, lo, hi, depth):
    @pl.when(first)
    def _():
        def fill(i, carry):
            x = lo + i
            ref[x, FIRST:BASE, :] = jnp.broadcast_to(
                ref[x, BASE : BASE + 1, :], (BASE - FIRST, ref.shape[2])
            )
            return carry

        lax.fori_loop(0, hi - lo, fill, 0)

    @pl.when(last)
    def _():
        def fill(i, carry):
            x = lo + i
            top = BASE + depth
            ref[x, top : FIRST + SPAN, :] = jnp.broadcast_to(
                ref[x, top - 1 : top, :], (FIRST + SPAN - top, ref.shape[2])
            )
            return carry

        lax.fori_loop(0, hi - lo, fill, 0)


def one_side(positive, behind, forward):
    growing = jnp.maximum(jnp.maximum(behind, 0.0) ** 2, jnp.minimum(forward, 0.0) ** 2)
    falling = jnp.maximum(jnp.minimum(behind, 0.0) ** 2, jnp.maximum(forward, 0.0) ** 2)
    return jnp.where(positive, growing, falling)


def sweep(src, dst, lo, count):
    lanes = src.shape[2]

    def body(i, carry):
        x = lo + i
        for start, step_rows in LATE:
            start = start + 1
            lane = lax.broadcasted_iota(jnp.int32, (step_rows, lanes), 1)

            def at(x, shift=0, start=start, step_rows=step_rows):
                return src[x, start + shift : start + shift + step_rows, :]

            s = at(x)
            positive = s > 0
            sp = jnp.where(lane == lanes - 1, s, pltpu.roll(s, lanes - 1, 1))
            sm = jnp.where(lane == 0, s, pltpu.roll(s, 1, 1))
            total = one_side(positive, s - at(x - 1), at(x + 1) - s)
            total = total + one_side(positive, s - at(x, -1), at(x, 1) - s)
            total = total + one_side(positive, s - sm, sp - s)
            size = jnp.sqrt(total + gradient_eps)
            sign = s / jnp.sqrt(s * s + 1.0)
            dst[x, start : start + step_rows, :] = s - pseudo_step * sign * (size - 1.0)
        return carry

    lax.fori_loop(0, count, body, 0)


def ends(place_ref):
    first_x = place_ref[0] == 0
    last_x = place_ref[0] == place_ref[2] - 1
    first_z = place_ref[1] == 0
    last_z = place_ref[1] == place_ref[3] - 1
    return first_x, last_x, first_z, last_z


def inner_kernel(place_ref, scale_ref, u_ref, v_ref, w_ref, slots_ref, f0, f1):
    count, halves, _, lanes = slots_ref.shape
    own = halves * count
    _, _, first_z, last_z = ends(place_ref)
    for h in range(halves):

        def write(i, rows, value, h=h):
            f0[EDGE + h * count + i, rows, :] = value

        regroup(lambda n, at, h=h: slots_ref[n, h, at, :], count, lanes, range(count), write)
    coefs = (u_ref, v_ref, w_ref)
    stage(f0, None, f1, coefs, scale_ref, EDGE + 3, own - 6, (0.0, 1.0))
    clamp_rows(f1, first_z, last_z, EDGE + 3, EDGE + own - 3, lanes)


def outer_kernel(
    place_ref, scale_ref, u_ref, v_ref, w_ref, below_ref, above_ref, f0_in, f1_in,
    f0, f1, f2, up_ref, down_ref,
):
    del f0_in, f1_in
    count, _, lanes = below_ref.shape
    begin, end = EDGE, f0.shape[0] - EDGE
    first_x, last_x, first_z, last_z = ends(place_ref)
    for ref, at_plane, planes in (
        (below_ref, begin - count, range(count - 6, count)),
        (above_ref, end, range(6)),
    ):

        def write(i, rows, value, at_plane=at_plane):
            f0[at_plane + i, rows, :] = value

        regroup(lambda n, at, ref=ref: ref[n, at, :], count, lanes, planes, write)
    clamp_planes(f0, first_x, last_x, begin - 6, end + 6, begin, end)
    coefs = (u_ref, v_ref, w_ref)
    for lo, hi in ((begin - 3, begin + 3), (end - 3, end + 3)):
        stage(f0, None, f1, coefs, scale_ref, lo, hi - lo, (0.0, 1.0))
    clamp_planes(f1, first_x, last_x, begin - 3, end + 3, begin, end)
    for lo, hi in ((begin - 3, begin + 3), (end - 3, end + 3)):
        clamp_rows(f1, first_z, last_z, lo, hi, lanes)
    for lo, hi in ((begin, begin + HIGH), (end - LOW, end)):
        stage(f1, f0, f2, coefs, scale_ref, lo, hi - lo, (0.75, 0.25))
        clamp_rows(f2, first_z, last_z, lo, hi, lanes)
    for ref, start in ((up_ref, end - LOW), (down_ref, begin)):
        for i in range(ref.shape[0]):
            ref[i] = f2[start + i]


def third_kernel(place_ref, scale_ref, u_ref, v_ref, w_ref, f0, f1, f2_in, f2, f3):
    del f2_in
    _, _, first_z, last_z = ends(place_ref)
    begin, end = EDGE, f0.shape[0] - EDGE
    coefs = (u_ref, v_ref, w_ref)
    lo, hi = begin + HIGH, end - LOW
    stage(f1, f0, f2, coefs, scale_ref, lo, hi - lo, (0.75, 0.25))
    clamp_rows(f2, first_z, last_z, lo, hi, f2.shape[2])
    lo, hi = begin + 3, end - 3
    stage(f2, f0, f3, coefs, scale_ref, lo, hi - lo, (1.0 / 3.0, 2.0 / 3.0), LATE)


def last_kernel(
    place_ref, scale_ref, u_ref, v_ref, w_ref, below_ref, above_ref, f0, f2_in, f3_in,
    f2, f3, slots_ref, lower_ref, upper_ref, f4,
):
    del f2_in, f3_in
    begin, end = EDGE, f0.shape[0] - EDGE
    own, depth = end - begin, lower_ref.shape[2]
    first_x, last_x, first_z, last_z = ends(place_ref)
    for ref, start in ((below_ref, begin - LOW), (above_ref, end)):
        for i in range(ref.shape[0]):
            f2[start + i] = ref[i]
    clamp_planes(f2, first_x, last_x, begin - LOW, end + HIGH, begin, end)
    coefs = (u_ref, v_ref, w_ref)
    for lo, hi in ((begin - 1, begin + 3), (end - 3, end + 2)):
        stage(f2, f0, f3, coefs, scale_ref, lo, hi - lo, (1.0 / 3.0, 2.0 / 3.0), LATE)
    clamp_planes(f3, first_x, last_x, begin - 1, end + 2, begin, end)
    clamp_rows(f3, first_z, last_z, begin - 1, end + 2, depth)
    sweep(f3, f4, begin, own + 1)
    clamp_planes(f4, jnp.bool_(False), last_x, begin, end + 1, begin, end)
    clamp_rows(f4, jnp.bool_(False), last_z, begin, end + 1, depth)
    count = slots_ref.shape[0]
    piece = depth // count

    def turn(i, carry):
        lower = f4[begin + i, BASE : BASE + depth, :].T
        upper = f4[begin + i, BASE + 1 : BASE + 1 + depth, :].T
        for ref, value in ((lower_ref, lower), (upper_ref, upper)):
            ref[i, 0:depth, :] = value
            ref[i, depth : depth + 8, :] = jnp.broadcast_to(value[depth - 1 : depth], (8, depth))

        @pl.when(i < own)
        def _():
            for d in range(count):
                slots_ref[d, i] = lower[d * piece : (d + 1) * piece]

        return carry

    lax.fori_loop(0, own + 1, turn, 0)


def store_edge(refs, at, a, b):
    weight = 1.0 / (1.0 + jnp.exp2((sharpness * 1.4426950408889634) * (a * b)))
    low = a * a + crossing_bias
    part = low / (low + (b * b + crossing_bias))
    along = b - a
    scaled = weight * along
    for ref, value in zip(
        refs, (weight, part, scaled, scaled * along, weight * part, part * along), strict=True
    ):
        ref[at] = value


def add(old, new):
    return new if old is None else old + new


def contour_kernel(lower_ref, upper_ref, out_ref, *scratch):
    planes, _, lanes = lower_ref.shape
    depth = lanes
    sides = (lower_ref, upper_ref)
    x_edges, y_edges, z_edges = scratch[0:6], scratch[6:12], scratch[12:18]

    def across_edges(x, carry):
        for start in range(0, depth + 8, 8):
            at = slice(start, start + 8)
            store_edge(z_edges, (x, at), lower_ref[x, at, :], upper_ref[x, at, :])
            if start < depth:
                for n, ref in enumerate(sides):
                    there = ref[x, start + 1 : start + 9, :]
                    store_edge(y_edges, (n, x, at), ref[x, at, :], there)
        return carry

    lax.fori_loop(0, planes, across_edges, 0)

    def cubes(x, carry):
        for start in range(0, depth + 8, 8):
            at = slice(start, start + 8)
            for n, ref in enumerate(sides):
                store_edge(x_edges, (n, x, at), ref[x, at, :], ref[x + 1, at, :])
        for start in range(0, depth, 8):

            def rows(bit, start=start):
                return slice(start + bit, start + bit + 8)

            f = {}
            for bx in (0, 1):
                for by in (0, 1):
                    for bz in (0, 1):
                        f[bx, by, bz] = sides[bz][x + bx, rows(by), :]
            diff = {}
            for d in range(3):
                for key in sorted(f):
                    if key[d] == 0:
                        diff[d, key] = f[set_bit(key, d, 1)] - f[key]
            total = None
            mass = [None] * 3
            moment = {}
            target = [None] * 3
            twist = {}
            for d in range(3):
                a1, a2 = [a for a in range(3) if a != d]
                weights = {}
                for key in sorted(f):
                    if key[d] != 0:
                        continue
                    bx, by, bz = key
                    refs, at = (
                        (x_edges, (bz, x, rows(by))),
                        (y_edges, (bz, x + bx, rows(0))),
                        (z_edges, (x + bx, rows(by))),
                    )[d]
                    weight, part, scaled_d, square, moved, height = [ref[at] for ref in refs]
                    weights[key[a1], key[a2]] = weight
                    mass[d] = add(mass[d], moved)
                    normal = [None] * 3
                    normal[d] = diff[d, key]
                    scaled = [None] * 3
                    scaled[d] = scaled_d
                    projection = height
                    for a in (a1, a2):
                        low = diff[a, set_bit(key, a, 0)]
                        third = 3 - a - d
                        name = (third, key[third])
                        if name not in twist:
                            twist[name] = diff[a, set_bit(set_bit(key, a, 0), d, 1)] - low
                        normal[a] = low + part * twist[name]
                        scaled[a] = weight * normal[a]
                        if key[a] == 1:
                            projection = projection + normal[a]
                    for i in range(3):
                        for j in range(i, 3):
                            if i == d and j == d:
                                value = square
                            elif j == d:
                                value = scaled[j] * normal[i]
                            else:
                                value = scaled[i] * normal[j]
                            moment[i, j] = add(moment.get((i, j)), value)
                        target[i] = add(target[i], scaled[i] * projection)
                ends = weights[1, 0] + weights[1, 1]
                mass[a1] = add(mass[a1], ends)
                mass[a2] = add(mass[a2], weights[0, 1] + weights[1, 1])
                total = add(total, (weights[0, 0] + weights[0, 1]) + ends)
            inverse = tikhonov / (total + mass_prior)
            r0, r1, r2 = [target[i] + (mass[i] + 0.5 * mass_prior) * inverse for i in range(3)]
            over0 = 1.0 / (moment[0, 0] + tikhonov)
            l1 = moment[0, 1] * over0
            l2 = moment[0, 2] * over0
            over1 = 1.0 / ((moment[1, 1] + tikhonov) - l1 * moment[0, 1])
            rest = moment[1, 2] - l1 * moment[0, 2]
            l3 = rest * over1
            over2 = 1.0 / (((moment[2, 2] + tikhonov) - l2 * moment[0, 2]) - l3 * rest)
            r1 = r1 - l1 * r0
            r2 = (r2 - l2 * r0) - l3 * r1
            x2 = r2 * over2
            x1 = r1 * over1 - l3 * x2
            out_ref[0, x, rows(0), :] = (r0 * over0 - l1 * x1) - l2 * x2
            out_ref[1, x, rows(0), :] = x1
            out_ref[2, x, rows(0), :] = x2
        return carry

    lax.fori_loop(0, planes - 1, cubes, 0)


def set_bit(key, d, value):
    listed = list(key)
    listed[d] = value
    return tuple(listed)


def speeds(flow_amplitude, x_start, z_start, own, depth, total_x, total_y, total_z):
    def cells(start, count, total):
        return ((start + jnp.arange(count, dtype=jnp.int32)).astype(jnp.float32) + 0.5) / total

    x = cells(x_start - EDGE, EDGE + own + EDGE, total_x)
    y = cells(0, total_y, total_y)
    z = cells(z_start - BASE, ROWS, total_z)
    half_x, full_x = jnp.sin(jnp.pi * x) ** 2, jnp.sin(2.0 * jnp.pi * x)
    half_y, full_y = jnp.sin(jnp.pi * y) ** 2, jnp.sin(2.0 * jnp.pi * y)
    half_z, full_z = jnp.sin(jnp.pi * z) ** 2, jnp.sin(2.0 * jnp.pi * z)
    scale = jnp.stack(
        [
            flow_amplitude[0] * half_x,
            -0.5 * flow_amplitude[1] * full_x,
            -0.5 * flow_amplitude[2] * full_x,
        ]
    )
    u = full_z[:, None] * full_y[None, :]
    v = full_z[:, None] * half_y[None, :]
    w = half_z[:, None] * full_y[None, :]
    return scale, u, v, w


def near(value):
    return pltpu.with_memory_space_constraint(value, pltpu.VMEM)


def shards(level_set, flow_amplitude):
    own, cols, layers = level_set.shape
    count_x, count_z = lax.axis_size("px"), lax.axis_size("py")
    at_x, at_z = lax.axis_index("px"), lax.axis_index("py")
    depth, wide = layers // count_z, cols * count_z
    lanes = 128
    halves = own * cols // lanes
    f32 = jnp.float32
    slots = pl.pallas_call(
        pack_kernel,
        out_shape=pltpu.VMEM((count_z, halves, SLOT, lanes), f32),
        in_specs=[VMEM],
        out_specs=VMEM,
        scratch_shapes=[pltpu.VMEM((halves, layers + 32, lanes), f32)],
        compiler_params=PARAMS,
        name="pack",
    )(level_set.reshape(own * cols, layers))
    slots = lax.all_to_all(slots, "py", split_axis=0, concat_axis=0, tiled=True)
    ring = [(i, (i + 1) % count_x) for i in range(count_x)]
    back_ring = [(b, a) for a, b in ring]
    below = lax.ppermute(slots[:, halves - 1], "px", ring)
    above = lax.ppermute(slots[:, 0], "px", back_ring)
    scale, u, v, w = speeds(
        flow_amplitude, at_x * own, at_z * depth, own, depth, own * count_x, wide, layers
    )
    place = jnp.stack([at_x, at_z, jnp.int32(count_x), jnp.int32(count_z)]).astype(jnp.int32)
    planes = EDGE + own + EDGE
    field = pltpu.VMEM((planes, ROWS, wide), f32)
    coefs = [near(a) for a in (u, v, w)]
    f0, f1 = pl.pallas_call(
        inner_kernel,
        out_shape=[field, field],
        in_specs=[SMEM, SMEM] + [VMEM] * 4,
        out_specs=[VMEM] * 2,
        compiler_params=PARAMS,
        name="inner",
    )(place, scale, *coefs, near(slots))
    f0, f1, f2, up, down = pl.pallas_call(
        outer_kernel,
        out_shape=[field, field, field]
        + [pltpu.VMEM((n, ROWS, wide), f32) for n in (LOW, HIGH)],
        in_specs=[SMEM, SMEM] + [VMEM] * 7,
        out_specs=[VMEM] * 5,
        input_output_aliases={7: 0, 8: 1},
        compiler_params=PARAMS,
        name="outer",
    )(place, scale, *coefs, near(below), near(above), near(f0), near(f1))
    below = lax.ppermute(up, "px", ring)
    above = lax.ppermute(down, "px", back_ring)
    f2, f3 = pl.pallas_call(
        third_kernel,
        out_shape=[field, field],
        in_specs=[SMEM, SMEM] + [VMEM] * 6,
        out_specs=[VMEM] * 2,
        input_output_aliases={7: 0},
        compiler_params=PARAMS,
        name="third",
    )(place, scale, *coefs, near(f0), near(f1), near(f2))
    _, _, turned, lower, upper = pl.pallas_call(
        last_kernel,
        out_shape=[
            field,
            field,
            pltpu.VMEM((count_z, own, cols, depth), f32),
            pltpu.VMEM((own + 1, wide + 8, depth), f32),
            pltpu.VMEM((own + 1, wide + 8, depth), f32),
        ],
        in_specs=[SMEM, SMEM] + [VMEM] * 8,
        out_specs=[VMEM] * 5,
        scratch_shapes=[field],
        input_output_aliases={8: 0, 9: 1},
        compiler_params=PARAMS,
        name="last",
    )(place, scale, *coefs, near(below), near(above), near(f0), near(f2), near(f3))
    back = lax.all_to_all(turned, "py", split_axis=0, concat_axis=0, tiled=True)
    phi_next = jnp.moveaxis(back, 0, 2).reshape(own, cols, layers)
    vertices = pl.pallas_call(
        contour_kernel,
        out_shape=jax.ShapeDtypeStruct((3, own, wide, depth), f32),
        in_specs=[VMEM] * 2,
        out_specs=VMEM,
        scratch_shapes=[pltpu.VMEM((2, own, wide + 8, depth), f32)] * 6
        + [pltpu.VMEM((2, own + 1, wide, depth), f32)] * 6
        + [pltpu.VMEM((own + 1, wide + 8, depth), f32)] * 6,
        compiler_params=WIDE_PARAMS,
        name="contour",
    )(near(lower), near(upper))
    return (phi_next, vertices)


def solution(mesh):
    in_specs = (P("px", "py", None), P())
    out_specs = (P("px", "py", None), P(None, "px", None, "py"))
    return jax.shard_map(shards, mesh=mesh, in_specs=in_specs, out_specs=out_specs, check_vma=False)
```

time: 148 us -> 114 us (0.77)
  Pallas kernels: 92.3 us -> 68.8 us
  waiting for transfers between devices: 32.6 us -> 19.4 us
  starting transfers between devices: 13.9 us -> 17 us
  other arithmetic: 2.81 us -> 0.96 us
    ppermute x2 -> x4, waiting for transfers between devices: 16.1 us -> 2.4 us  [the longest x1 2.4 us: shards(): above = lax.ppermute(slots[:, 0], 'px', back_ring)]
    pallas_call x1, Pallas kernels: 31.6 us -> 18 us  [shards(): pl.pallas_call(contour_kernel, out_shape=jax.ShapeDtypeStruct((3, own, wi...]
    pallas_call x3 -> x5, Pallas kernels: 60.8 us -> 50.8 us  [the longest x1 17 us: shards(): pl.pallas_call(outer_kernel, out_shape=[field, field, field] + [pltpu.VME...]
    ppermute x2 -> x4, starting transfers between devices: 4.83 us -> 8.07 us  [the longest x1 3.24 us: shards(): below = lax.ppermute(up, 'px', ring)]
  transfers between devices with their start and end apart: 4 -> 6, of which waited for: 3 -> 2; matrix products, arithmetic and copies ran while one was open for 2% -> 1% of each run, Pallas kernels for 21% -> 35%
where the time goes in v2:
time: 114 us; the launch traced here: 112 us
  Pallas kernels  68.8 us (60%)
  waiting for transfers between devices  19.4 us (17%)
  starting transfers between devices  17 us (15%)
  local copies, waits for them, and re-layouts  3.83 us (3%)
  between operations  2.02 us (2%)
    pallas_call x1, Pallas kernels, shards(): pl.pallas_call(contour_kernel, out_shape=jax.ShapeDtypeStruct((3, own, wi...  18 us
    all_to_all x1, waiting for transfers between devices, shards(): slots = lax.all_to_all(slots, 'py', split_axis=0, concat_axis=0, tiled=True)  17 us
    pallas_call x1, Pallas kernels, shards(): pl.pallas_call(outer_kernel, out_shape=[field, field, field] + [pltpu.VME...  17 us
    pallas_call x1, Pallas kernels, shards(): pl.pallas_call(last_kernel, out_shape=[field, field, pltpu.VMEM((count_z,...  11.5 us
    pallas_call x1, Pallas kernels, shards(): pl.pallas_call(inner_kernel, out_shape=[field, field], in_specs=[SMEM, SM...  10.9 us
    pallas_call x1, Pallas kernels, shards(): pl.pallas_call(third_kernel, out_shape=[field, field], in_specs=[SMEM, SM...  9.93 us
    all_to_all x1, starting transfers between devices, shards(): slots = lax.all_to_all(slots, 'py', split_axis=0, concat_axis=0, tiled=True)  5.37 us
    all_to_all x1, starting transfers between devices, shards(): back = lax.all_to_all(turned, 'py', split_axis=0, concat_axis=0, tiled=True)  3.56 us
  transfers between devices with their start and end apart: 6, of which 2 were waited for; matrix products, arithmetic and copies ran while one was open for 1% of the time, Pallas kernels for 35%

profile of v2, /device:TPU:9, one launch (start us, length us, event | category | flops | bytes accessed | tf_op | source)
XLA Modules:
  0.0 112.1 jit_solution(18441084213974065229)
XLA Ops:
  0.6 0.0 copy-start.1
  0.6 0.0 copy-start
  0.6 1.2 %copy-done = f32[16,16,1024]{2,1,0:T(8,128)S(1)} copy-done((f32[16,16,1024]{2,1,0:T(8,128)S(1)}, f32[16,16,1024]{2,1,0:T(8,128)}, u32[]{:S(2)}) %copy-start) | copy-done | bytes 1048600
  1.9 1.5 %pack.1 = f32[8,2,152,128]{3,2,1,0:T(8,128)} custom-call(f32[256,1024]{1,0:T(8,128)S(1)} %bitcast.20), custom_call_target="tpu_custom_call" | custom-call | tf_op jit(solution)/shard_map/pack/pallas_call | solution.py:492
  3.4 5.4 %all-to-all-start = ((f32[8,2,152,128]{3,2,1,0:T(8,128)}), f32[8,2,152,128]{3,2,1,0:T(8,128)S(1)}, u32[]{:S(2)}, u32[]{:S(2)}) async-start(f32[8,2,152,128]{3,2,1,0:T(8,128)} %pack.1), calls=%async_computation | async-start | bytes 2490368 | tf_op jit(solution)/shard_map/all_to_all | solution.py:501
  8.7 0.0 copy-done.1
  8.7 0.6 fusion
  10.0 0.1 broadcast_multiply_fusion.4
  10.0 0.1 sine_multiply_fusion.1
  10.1 17.0 %all-to-all-done.slots_ref = f32[8,2,152,128]{3,2,1,0:T(8,128)S(1)} async-done(((f32[8,2,152,128]{3,2,1,0:T(8,128)}), f32[8,2,152,128]{3,2,1,0:T(8,128)S(1)}, u32[]{:S(2)}, u32[]{:S(2)}) %all-to-all-start) | async-done | bytes 1245216 | tf_op jit(solution)/shard_map/all_to_all | solution.py:501
  27.1 0.9 slice_bitcast_fusion
  28.0 1.6 %collective-permute-start.1 = (f32[8,152,128]{2,1,0:T(8,128)}, f32[8,152,128]{2,1,0:T(8,128)S(1)}, u32[]{:S(2)}, u32[]{:S(2)}) collective-permute-start(f32[8,152,128]{2,1,0:T(8,128)} %get-tuple-element.26), channel_id=1, source_target_pairs={{8,0},{16,8},{24,16},{32,24},{40,32},{48,40},{56,48},{64,56},{72,6... | collective-permute-start | bytes 1867784 | tf_op jit(solution)/shard_map/ppermute | solution.py:505
  29.6 3.2 %collective-permute-start = (f32[8,152,128]{2,1,0:T(8,128)S(1)}, f32[8,152,128]{2,1,0:T(8,128)S(1)}, u32[]{:S(2)}, u32[]{:S(2)}) collective-permute-start(f32[8,152,128]{2,1,0:T(8,128)S(1)} %get-tuple-element.27), channel_id=1, source_target_pairs={{0,8},{8,16},{16,24},{24,32},{32,40},{40,48},{48,56},{56,64},{64,7... | collective-permute-start | bytes 1867784 | tf_op jit(solution)/shard_map/ppermute | solution.py:504
  32.8 0.1 pad_add_fusion.place_ref
  33.5 0.6 multiply_multiply_fusion
  34.1 0.1 sine_multiply_fusion
  34.2 0.1 broadcast_multiply_fusion.1
  34.3 10.9 %inner.1 = (f32[32,160,128]{2,1,0:T(8,128)S(1)}, f32[32,160,128]{2,1,0:T(8,128)S(1)}) custom-call(s32[4]{0:T(128)S(1)} %pad_add_fusion.place_ref, f32[3,32]{1,0:T(4,128)S(1)} %pad_maximum_fusion.scale_ref, f32[160,128]{1,0:T(8,128)S(1)} %get-tuple-element.29.u_ref, f32[160,128]{1,0:T(8,128)S(1)} %get-tuple-element.28.v_ref, ...), custom_call_target="tpu_custom_call" | custom-call | tf_op jit(solution)/shard_map/inner/pallas_call | solution.py:513
  45.2 2.4 %collective-permute-done.1.above_ref = f32[8,152,128]{2,1,0:T(8,128)S(1)} collective-permute-done((f32[8,152,128]{2,1,0:T(8,128)}, f32[8,152,128]{2,1,0:T(8,128)S(1)}, u32[]{:S(2)}, u32[]{:S(2)}) %collective-permute-start.1) | collective-permute-done | bytes 622624 | tf_op jit(solution)/shard_map/ppermute | solution.py:505
  47.6 0.0 collective-permute-done.below_ref
  47.6 17.0 %outer.1 = (f32[32,160,128]{2,1,0:T(8,128)S(1)}, f32[32,160,128]{2,1,0:T(8,128)S(1)}, f32[32,160,128]{2,1,0:T(8,128)S(1)}, f32[4,160,128]{2,1,0:T(8,128)S(1)}, f32[5,160,128]{2,1,0:T(8,128)S(1)}) custom-call(s32[4]{0:T(128)S(1)} %pad_add_fusion.place_ref, f32[3,32]{1,0:T(4,128)S(1)} %pad_maximum_fusion.scale_ref, ...), custom_call_target="tpu_custom_call", output_to_operand_aliasing={{0}: (7, {}), {1}: (8, {})} | custom-call | tf_op jit(solution)/shard_map/outer/pallas_call | solution.py:521
  64.6 0.1 collective-permute-start.3
  64.7 3.2 %collective-permute-start.2 = (f32[4,160,128]{2,1,0:T(8,128)S(1)}, f32[4,160,128]{2,1,0:T(8,128)S(1)}, u32[]{:S(2)}, u32[]{:S(2)}) collective-permute-start(f32[4,160,128]{2,1,0:T(8,128)S(1)} %get-tuple-element.16), channel_id=1, source_target_pairs={{0,8},{8,16},{16,24},{24,32},{32,40},{40,48},{48,56},{56,64},{64,7... | collective-permute-start | bytes 983048 | tf_op jit(solution)/shard_map/ppermute | solution.py:531
  67.9 9.9 %third.1 = (f32[32,160,128]{2,1,0:T(8,128)S(1)}, f32[32,160,128]{2,1,0:T(8,128)S(1)}) custom-call(s32[4]{0:T(128)S(1)} %pad_add_fusion.place_ref, f32[3,32]{1,0:T(4,128)S(1)} %pad_maximum_fusion.scale_ref, f32[160,128]{1,0:T(8,128)S(1)} %get-tuple-element.29.u_ref, f32[160,128]{1,0:T(8,128)S(1)} %get-tuple-element.28.v_ref, ...), custom_call_target="tpu_custom_call", output_to_operand_aliasing={{0}: (7, {})} | custom-call | tf_op jit(solution)/shard_map/third/pallas_call | solution.py:533
  77.8 0.0 collective-permute-done.2.below_ref
  77.9 0.0 collective-permute-done.3.above_ref
  77.9 11.5 %last.1 = (f32[32,160,128]{2,1,0:T(8,128)S(1)}, f32[32,160,128]{2,1,0:T(8,128)S(1)}, f32[8,16,16,128]{3,2,1,0:T(8,128)}, f32[17,136,128]{2,1,0:T(8,128)S(1)}, f32[17,136,128]{2,1,0:T(8,128)S(1)}) custom-call(s32[4]{0:T(128)S(1)} %pad_add_fusion.place_ref, f32[3,32]{1,0:T(4,128)S(1)} %pad_maximum_fusion.scale_ref, ...), custom_call_target="tpu_custom_call", output_to_operand_aliasing={{0}: (8, {}), {1}: (9, {})} | custom-call | tf_op jit(solution)/shard_map/last/pallas_call | solution.py:542
  89.4 3.6 %all-to-all-start.1 = ((f32[8,16,16,128]{3,2,1,0:T(8,128)}), f32[8,16,16,128]{3,2,1,0:T(8,128)S(1)}, u32[]{:S(2)}, u32[]{:S(2)}) async-start(f32[8,16,16,128]{3,2,1,0:T(8,128)} %get-tuple-element.23), calls=%async_computation.1 | async-start | bytes 2097152 | tf_op jit(solution)/shard_map/all_to_all | solution.py:558
  93.0 18.0 %contour.1 = f32[3,16,128,128]{3,2,1,0:T(8,128)} custom-call(f32[17,136,128]{2,1,0:T(8,128)S(1)} %get-tuple-element.24.lower_ref, f32[17,136,128]{2,1,0:T(8,128)S(1)} %get-tuple-element.25.upper_ref), custom_call_target="tpu_custom_call" | custom-call | tf_op jit(solution)/shard_map/contour/pallas_call | solution.py:560
  111.0 0.0 all-to-all-done.1
  111.0 1.1 copy_bitcast_fusion
  (1 shorter events, 0.0 us)
Async XLA Ops:
  0.6 8.1 %copy-start.1 = (f32[3]{0:T(128)S(1)}, f32[3]{0:T(128)}, u32[]{:S(2)}) copy-start(f32[3]{0:T(128)} %param.3) | copy-start | bytes 40
  0.6 1.2 %copy-start = (f32[16,16,1024]{2,1,0:T(8,128)S(1)}, f32[16,16,1024]{2,1,0:T(8,128)}, u32[]{:S(2)}) copy-start(f32[16,16,1024]{2,1,0:T(8,128)} %param.2) | copy-start | bytes 3145732
  3.4 23.7 %all-to-all-start = ((f32[8,2,152,128]{3,2,1,0:T(8,128)}), f32[8,2,152,128]{3,2,1,0:T(8,128)S(1)}, u32[]{:S(2)}, u32[]{:S(2)}) async-start(f32[8,2,152,128]{3,2,1,0:T(8,128)} %pack.1), calls=%async_computation | async-start | bytes 2490368 | tf_op jit(solution)/shard_map/all_to_all | solution.py:501
  28.0 19.6 %collective-permute-start.1 = (f32[8,152,128]{2,1,0:T(8,128)}, f32[8,152,128]{2,1,0:T(8,128)S(1)}, u32[]{:S(2)}, u32[]{:S(2)}) collective-permute-start(f32[8,152,128]{2,1,0:T(8,128)} %get-tuple-element.26), channel_id=1, source_target_pairs={{8,0},{16,8},{24,16},{32,24},{40,32},{48,40},{56,48},{64,56},{72,6... | collective-permute-start | bytes 1867784 | tf_op jit(solution)/shard_map/ppermute | solution.py:505
  29.6 18.0 %collective-permute-start = (f32[8,152,128]{2,1,0:T(8,128)S(1)}, f32[8,152,128]{2,1,0:T(8,128)S(1)}, u32[]{:S(2)}, u32[]{:S(2)}) collective-permute-start(f32[8,152,128]{2,1,0:T(8,128)S(1)} %get-tuple-element.27), channel_id=1, source_target_pairs={{0,8},{8,16},{16,24},{24,32},{32,40},{40,48},{48,56},{56,64},{64,7... | collective-permute-start | bytes 1867784 | tf_op jit(solution)/shard_map/ppermute | solution.py:504
  64.6 13.3 %collective-permute-start.3 = (f32[5,160,128]{2,1,0:T(8,128)S(1)}, f32[5,160,128]{2,1,0:T(8,128)S(1)}, u32[]{:S(2)}, u32[]{:S(2)}) collective-permute-start(f32[5,160,128]{2,1,0:T(8,128)S(1)} %get-tuple-element.17), channel_id=1, source_target_pairs={{8,0},{16,8},{24,16},{32,24},{40,32},{48,40},{56,48},{64,56},{72,6... | collective-permute-start | bytes 1228808 | tf_op jit(solution)/shard_map/ppermute | solution.py:532
  64.7 13.2 %collective-permute-start.2 = (f32[4,160,128]{2,1,0:T(8,128)S(1)}, f32[4,160,128]{2,1,0:T(8,128)S(1)}, u32[]{:S(2)}, u32[]{:S(2)}) collective-permute-start(f32[4,160,128]{2,1,0:T(8,128)S(1)} %get-tuple-element.16), channel_id=1, source_target_pairs={{0,8},{8,16},{16,24},{24,32},{32,40},{40,48},{48,56},{56,64},{64,7... | collective-permute-start | bytes 983048 | tf_op jit(solution)/shard_map/ppermute | solution.py:531
  89.4 21.6 %all-to-all-start.1 = ((f32[8,16,16,128]{3,2,1,0:T(8,128)}), f32[8,16,16,128]{3,2,1,0:T(8,128)S(1)}, u32[]{:S(2)}, u32[]{:S(2)}) async-start(f32[8,16,16,128]{3,2,1,0:T(8,128)} %get-tuple-element.23), calls=%async_computation.1 | async-start | bytes 2097152 | tf_op jit(solution)/shard_map/all_to_all | solution.py:558

commit v3 on v2

--- a/solution.py
+++ b/solution.py
@@ -17,11 +17,12 @@
 LOW, HIGH = 4, 5
 SHIFT, SLOT = 13, 152
 BASE, ROWS, FIRST, SPAN, STEP = 15, 160, 8, 144, 48
+PASS = 32
 LATE = ((14, 48), (62, 48), (110, 40))
 VMEM = pl.BlockSpec(memory_space=pltpu.VMEM)
 SMEM = pl.BlockSpec(memory_space=pltpu.SMEM)
 PARAMS = pltpu.CompilerParams(vmem_limit_bytes=24 * 1024 * 1024)
-WIDE_PARAMS = pltpu.CompilerParams(vmem_limit_bytes=48 * 1024 * 1024)
+WIDE_PARAMS = pltpu.CompilerParams(vmem_limit_bytes=26 * 1024 * 1024)
 
 
 def pack_kernel(x_ref, out_ref, tall):
@@ -45,23 +46,25 @@
 
 def regroup(read, count, lanes, planes, write):
     group = lanes // count
-    index = lax.broadcasted_iota(jnp.int32, (8, lanes), 1) // group
-    for t in range(SLOT // 8):
-        at = slice(t * 8, t * 8 + 8)
-        v = [read(n, at) for n in range(count)]
+    for first in range(0, SLOT, PASS):
+        rows = min(PASS, SLOT - first)
+        index = lax.broadcasted_iota(jnp.int32, (rows, lanes), 1) // group
+        v = [read(n, slice(first, first + rows)) for n in range(count)]
         k = count // 2
         while k:
             low_part = (index & k) == 0
-            for i in range(count):
-                if i & k:
-                    continue
-                a, b = v[i], v[i | k]
-                v[i] = jnp.where(low_part, a, pltpu.roll(b, k * group, 1))
-                v[i | k] = jnp.where(low_part, pltpu.roll(a, lanes - k * group, 1), b)
+            pairs = [(i, i | k) for i in range(count) if not i & k]
+            moved = [
+                (pltpu.roll(v[j], k * group, 1), pltpu.roll(v[i], lanes - k * group, 1))
+                for i, j in pairs
+            ]
+            for (i, j), (from_j, from_i) in zip(pairs, moved, strict=True):
+                v[i] = jnp.where(low_part, v[i], from_j)
+                v[j] = jnp.where(low_part, from_i, v[j])
             k //= 2
-        start = BASE - SHIFT + t * 8
+        start = BASE - SHIFT + first
         for i in planes:
-            write(i, slice(start, start + 8), v[i])
+            write(i, slice(start, start + rows), v[i])
 
 
 def one_sided(pm2, pm1, p0, pp1, pp2, positive):
@@ -184,10 +187,11 @@
         lax.fori_loop(0, hi - lo, fill, 0)
 
 
-def one_side(positive, behind, forward):
-    growing = jnp.maximum(jnp.maximum(behind, 0.0) ** 2, jnp.minimum(forward, 0.0) ** 2)
-    falling = jnp.maximum(jnp.minimum(behind, 0.0) ** 2, jnp.maximum(forward, 0.0) ** 2)
-    return jnp.where(positive, growing, falling)
+def one_side(positive, s, behind, ahead):
+    drop = s - jnp.minimum(behind, ahead)
+    rise = jnp.maximum(behind, ahead) - s
+    steep = jnp.maximum(jnp.where(positive, drop, rise), 0.0)
+    return steep * steep
 
 
 def sweep(src, dst, lo, count):
@@ -206,11 +210,12 @@
             positive = s > 0
             sp = jnp.where(lane == lanes - 1, s, pltpu.roll(s, lanes - 1, 1))
             sm = jnp.where(lane == 0, s, pltpu.roll(s, 1, 1))
-            total = one_side(positive, s - at(x - 1), at(x + 1) - s)
-            total = total + one_side(positive, s - at(x, -1), at(x, 1) - s)
-            total = total + one_side(positive, s - sm, sp - s)
-            size = jnp.sqrt(total + gradient_eps)
-            sign = s / jnp.sqrt(s * s + 1.0)
+            total = one_side(positive, s, at(x - 1), at(x + 1))
+            total = total + one_side(positive, s, at(x, -1), at(x, 1))
+            total = total + one_side(positive, s, sm, sp)
+            total = total + gradient_eps
+            size = total * lax.rsqrt(total)
+            sign = s * lax.rsqrt(s * s + 1.0)
             dst[x, start : start + step_rows, :] = s - pseudo_step * sign * (size - 1.0)
         return carry
 
@@ -356,13 +361,15 @@
                     store_edge(y_edges, (n, x, at), ref[x, at, :], there)
         return carry
 
-    lax.fori_loop(0, planes, across_edges, 0)
-
-    def cubes(x, carry):
+    @pl.when(pl.program_id(0) == 0)
+    def _():
+        lax.fori_loop(0, planes, across_edges, 0)
+
+    def cubes(x):
         for start in range(0, depth + 8, 8):
             at = slice(start, start + 8)
             for n, ref in enumerate(sides):
-                store_edge(x_edges, (n, x, at), ref[x, at, :], ref[x + 1, at, :])
+                store_edge(x_edges, (n, at), ref[x, at, :], ref[x + 1, at, :])
         for start in range(0, depth, 8):
 
             def rows(bit, start=start):
@@ -391,7 +398,7 @@
                         continue
                     bx, by, bz = key
                     refs, at = (
-                        (x_edges, (bz, x, rows(by))),
+                        (x_edges, (bz, rows(by))),
                         (y_edges, (bz, x + bx, rows(0))),
                         (z_edges, (x + bx, rows(by))),
                     )[d]
@@ -440,12 +447,11 @@
             r2 = (r2 - l2 * r0) - l3 * r1
             x2 = r2 * over2
             x1 = r1 * over1 - l3 * x2
-            out_ref[0, x, rows(0), :] = (r0 * over0 - l1 * x1) - l2 * x2
-            out_ref[1, x, rows(0), :] = x1
-            out_ref[2, x, rows(0), :] = x2
-        return carry
-
-    lax.fori_loop(0, planes - 1, cubes, 0)
+            out_ref[0, 0, rows(0), :] = (r0 * over0 - l1 * x1) - l2 * x2
+            out_ref[1, 0, rows(0), :] = x1
+            out_ref[2, 0, rows(0), :] = x2
+
+    cubes(pl.program_id(0))
 
 
 def set_bit(key, d, value):
@@ -499,14 +505,14 @@
         name="pack",
     )(level_set.reshape(own * cols, layers))
     slots = lax.all_to_all(slots, "py", split_axis=0, concat_axis=0, tiled=True)
+    scale, u, v, w = speeds(
+        flow_amplitude, at_x * own, at_z * depth, own, depth, own * count_x, wide, layers
+    )
+    place = jnp.stack([at_x, at_z, jnp.int32(count_x), jnp.int32(count_z)]).astype(jnp.int32)
     ring = [(i, (i + 1) % count_x) for i in range(count_x)]
     back_ring = [(b, a) for a, b in ring]
     below = lax.ppermute(slots[:, halves - 1], "px", ring)
     above = lax.ppermute(slots[:, 0], "px", back_ring)
-    scale, u, v, w = speeds(
-        flow_amplitude, at_x * own, at_z * depth, own, depth, own * count_x, wide, layers
-    )
-    place = jnp.stack([at_x, at_z, jnp.int32(count_x), jnp.int32(count_z)]).astype(jnp.int32)
     planes = EDGE + own + EDGE
     field = pltpu.VMEM((planes, ROWS, wide), f32)
     coefs = [near(a) for a in (u, v, w)]
@@ -560,9 +566,10 @@
     vertices = pl.pallas_call(
         contour_kernel,
         out_shape=jax.ShapeDtypeStruct((3, own, wide, depth), f32),
+        grid=(own,),
         in_specs=[VMEM] * 2,
-        out_specs=VMEM,
-        scratch_shapes=[pltpu.VMEM((2, own, wide + 8, depth), f32)] * 6
+        out_specs=pl.BlockSpec((3, 1, wide, depth), lambda i: (0, i, 0, 0)),
+        scratch_shapes=[pltpu.VMEM((2, wide + 8, depth), f32)] * 6
         + [pltpu.VMEM((2, own + 1, wide, depth), f32)] * 6
         + [pltpu.VMEM((own + 1, wide + 8, depth), f32)] * 6,
         compiler_params=WIDE_PARAMS,

time: 114 us -> 109 us (0.956)
  Pallas kernels: 68.8 us -> 61.6 us
  waiting for transfers between devices: 19.4 us -> 22.4 us
    pallas_call x1, Pallas kernels: 10.9 us -> 7.87 us  [shards(): pl.pallas_call(inner_kernel, out_shape=[field, field], in_specs=[SMEM, SM...]
    ppermute x1, waiting for transfers between devices: 2.4 us -> 5.4 us  [shards(): above = lax.ppermute(slots[:, 0], 'px', back_ring)]
    pallas_call x1, Pallas kernels: 17 us -> 14.3 us  [shards(): pl.pallas_call(outer_kernel, out_shape=[field, field, field] + [pltpu.VME...]
  transfers between devices with their start and end apart: 6 -> 6, of which waited for: 2 -> 2; matrix products, arithmetic and copies ran while one was open for 1% -> 1% of each run, Pallas kernels for 35% -> 33%
where the time goes in v3:
time: 109 us; the launch traced here: 108 us
  Pallas kernels  61.6 us (57%)
  waiting for transfers between devices  22.4 us (21%)
  starting transfers between devices  17 us (16%)
  local copies, waits for them, and re-layouts  3.83 us (4%)
  between operations  2.02 us (2%)
    pallas_call x1, Pallas kernels, shards(): pl.pallas_call(contour_kernel, out_shape=jax.ShapeDtypeStruct((3, own, wi...  17.3 us
    all_to_all x1, waiting for transfers between devices, shards(): slots = lax.all_to_all(slots, 'py', split_axis=0, concat_axis=0, tiled=True)  17 us
    pallas_call x1, Pallas kernels, shards(): pl.pallas_call(outer_kernel, out_shape=[field, field, field] + [pltpu.VME...  14.3 us
    pallas_call x1, Pallas kernels, shards(): pl.pallas_call(last_kernel, out_shape=[field, field, pltpu.VMEM((count_z,...  10.7 us
    pallas_call x1, Pallas kernels, shards(): pl.pallas_call(third_kernel, out_shape=[field, field], in_specs=[SMEM, SM...  9.93 us
    pallas_call x1, Pallas kernels, shards(): pl.pallas_call(inner_kernel, out_shape=[field, field], in_specs=[SMEM, SM...  7.87 us
    ppermute x1, waiting for transfers between devices, shards(): above = lax.ppermute(slots[:, 0], 'px', back_ring)  5.4 us
    all_to_all x1, starting transfers between devices, shards(): slots = lax.all_to_all(slots, 'py', split_axis=0, concat_axis=0, tiled=True)  5.37 us
  transfers between devices with their start and end apart: 6, of which 2 were waited for; matrix products, arithmetic and copies ran while one was open for 1% of the time, Pallas kernels for 33%

profile of v3, /device:TPU:9, one launch (start us, length us, event | category | flops | bytes accessed | tf_op | source)
XLA Modules:
  0.0 107.9 jit_solution(12340088173619119749)
XLA Ops:
  0.6 0.0 copy-start.1
  0.6 0.0 copy-start
  0.6 1.2 %copy-done = f32[16,16,1024]{2,1,0:T(8,128)S(1)} copy-done((f32[16,16,1024]{2,1,0:T(8,128)S(1)}, f32[16,16,1024]{2,1,0:T(8,128)}, u32[]{:S(2)}) %copy-start) | copy-done | bytes 1048600
  1.9 1.5 %pack.1 = f32[8,2,152,128]{3,2,1,0:T(8,128)} custom-call(f32[256,1024]{1,0:T(8,128)S(1)} %bitcast.20), custom_call_target="tpu_custom_call" | custom-call | tf_op jit(solution)/shard_map/pack/pallas_call | solution.py:498
  3.4 5.4 %all-to-all-start = ((f32[8,2,152,128]{3,2,1,0:T(8,128)}), f32[8,2,152,128]{3,2,1,0:T(8,128)S(1)}, u32[]{:S(2)}, u32[]{:S(2)}) async-start(f32[8,2,152,128]{3,2,1,0:T(8,128)} %pack.1), calls=%async_computation | async-start | bytes 2490368 | tf_op jit(solution)/shard_map/all_to_all | solution.py:507
  8.7 0.0 copy-done.1
  8.7 0.6 fusion
  10.0 0.1 broadcast_multiply_fusion.4
  10.0 0.1 sine_multiply_fusion.1
  10.1 17.0 %all-to-all-done.slots_ref = f32[8,2,152,128]{3,2,1,0:T(8,128)S(1)} async-done(((f32[8,2,152,128]{3,2,1,0:T(8,128)}), f32[8,2,152,128]{3,2,1,0:T(8,128)S(1)}, u32[]{:S(2)}, u32[]{:S(2)}) %all-to-all-start) | async-done | bytes 1245216 | tf_op jit(solution)/shard_map/all_to_all | solution.py:507
  27.1 0.9 slice_bitcast_fusion
  28.0 1.6 %collective-permute-start.1 = (f32[8,152,128]{2,1,0:T(8,128)}, f32[8,152,128]{2,1,0:T(8,128)S(1)}, u32[]{:S(2)}, u32[]{:S(2)}) collective-permute-start(f32[8,152,128]{2,1,0:T(8,128)} %get-tuple-element.26), channel_id=1, source_target_pairs={{8,0},{16,8},{24,16},{32,24},{40,32},{48,40},{56,48},{64,56},{72,6... | collective-permute-start | bytes 1867784 | tf_op jit(solution)/shard_map/ppermute | solution.py:515
  29.6 3.2 %collective-permute-start = (f32[8,152,128]{2,1,0:T(8,128)S(1)}, f32[8,152,128]{2,1,0:T(8,128)S(1)}, u32[]{:S(2)}, u32[]{:S(2)}) collective-permute-start(f32[8,152,128]{2,1,0:T(8,128)S(1)} %get-tuple-element.27), channel_id=1, source_target_pairs={{0,8},{8,16},{16,24},{24,32},{32,40},{40,48},{48,56},{56,64},{64,7... | collective-permute-start | bytes 1867784 | tf_op jit(solution)/shard_map/ppermute | solution.py:514
  32.8 0.1 pad_add_fusion.place_ref
  33.5 0.6 multiply_multiply_fusion
  34.1 0.1 sine_multiply_fusion
  34.2 0.1 broadcast_multiply_fusion.1
  34.3 7.9 %inner.1 = (f32[32,160,128]{2,1,0:T(8,128)S(1)}, f32[32,160,128]{2,1,0:T(8,128)S(1)}) custom-call(s32[4]{0:T(128)S(1)} %pad_add_fusion.place_ref, f32[3,32]{1,0:T(4,128)S(1)} %pad_maximum_fusion.scale_ref, f32[160,128]{1,0:T(8,128)S(1)} %get-tuple-element.29.u_ref, f32[160,128]{1,0:T(8,128)S(1)} %get-tuple-element.28.v_ref, ...), custom_call_target="tpu_custom_call" | custom-call | tf_op jit(solution)/shard_map/inner/pallas_call | solution.py:519
  42.2 5.4 %collective-permute-done.1.above_ref = f32[8,152,128]{2,1,0:T(8,128)S(1)} collective-permute-done((f32[8,152,128]{2,1,0:T(8,128)}, f32[8,152,128]{2,1,0:T(8,128)S(1)}, u32[]{:S(2)}, u32[]{:S(2)}) %collective-permute-start.1) | collective-permute-done | bytes 622624 | tf_op jit(solution)/shard_map/ppermute | solution.py:515
  47.6 0.0 collective-permute-done.below_ref
  47.6 14.3 %outer.1 = (f32[32,160,128]{2,1,0:T(8,128)S(1)}, f32[32,160,128]{2,1,0:T(8,128)S(1)}, f32[32,160,128]{2,1,0:T(8,128)S(1)}, f32[4,160,128]{2,1,0:T(8,128)S(1)}, f32[5,160,128]{2,1,0:T(8,128)S(1)}) custom-call(s32[4]{0:T(128)S(1)} %pad_add_fusion.place_ref, f32[3,32]{1,0:T(4,128)S(1)} %pad_maximum_fusion.scale_ref, ...), custom_call_target="tpu_custom_call", output_to_operand_aliasing={{0}: (7, {}), {1}: (8, {})} | custom-call | tf_op jit(solution)/shard_map/outer/pallas_call | solution.py:527
  61.9 0.1 collective-permute-start.3
  62.0 3.2 %collective-permute-start.2 = (f32[4,160,128]{2,1,0:T(8,128)S(1)}, f32[4,160,128]{2,1,0:T(8,128)S(1)}, u32[]{:S(2)}, u32[]{:S(2)}) collective-permute-start(f32[4,160,128]{2,1,0:T(8,128)S(1)} %get-tuple-element.16), channel_id=1, source_target_pairs={{0,8},{8,16},{16,24},{24,32},{32,40},{40,48},{48,56},{56,64},{64,7... | collective-permute-start | bytes 983048 | tf_op jit(solution)/shard_map/ppermute | solution.py:537
  65.2 9.9 %third.1 = (f32[32,160,128]{2,1,0:T(8,128)S(1)}, f32[32,160,128]{2,1,0:T(8,128)S(1)}) custom-call(s32[4]{0:T(128)S(1)} %pad_add_fusion.place_ref, f32[3,32]{1,0:T(4,128)S(1)} %pad_maximum_fusion.scale_ref, f32[160,128]{1,0:T(8,128)S(1)} %get-tuple-element.29.u_ref, f32[160,128]{1,0:T(8,128)S(1)} %get-tuple-element.28.v_ref, ...), custom_call_target="tpu_custom_call", output_to_operand_aliasing={{0}: (7, {})} | custom-call | tf_op jit(solution)/shard_map/third/pallas_call | solution.py:539
  75.1 0.0 collective-permute-done.2.below_ref
  75.2 0.0 collective-permute-done.3.above_ref
  75.2 10.7 %last.1 = (f32[32,160,128]{2,1,0:T(8,128)S(1)}, f32[32,160,128]{2,1,0:T(8,128)S(1)}, f32[8,16,16,128]{3,2,1,0:T(8,128)}, f32[17,136,128]{2,1,0:T(8,128)S(1)}, f32[17,136,128]{2,1,0:T(8,128)S(1)}) custom-call(s32[4]{0:T(128)S(1)} %pad_add_fusion.place_ref, f32[3,32]{1,0:T(4,128)S(1)} %pad_maximum_fusion.scale_ref, ...), custom_call_target="tpu_custom_call", output_to_operand_aliasing={{0}: (8, {}), {1}: (9, {})} | custom-call | tf_op jit(solution)/shard_map/last/pallas_call | solution.py:548
  85.9 3.6 %all-to-all-start.1 = ((f32[8,16,16,128]{3,2,1,0:T(8,128)}), f32[8,16,16,128]{3,2,1,0:T(8,128)S(1)}, u32[]{:S(2)}, u32[]{:S(2)}) async-start(f32[8,16,16,128]{3,2,1,0:T(8,128)} %get-tuple-element.23), calls=%async_computation.1 | async-start | bytes 2097152 | tf_op jit(solution)/shard_map/all_to_all | solution.py:564
  89.5 17.3 %contour.1 = f32[3,16,128,128]{3,2,1,0:T(8,128)} custom-call(f32[17,136,128]{2,1,0:T(8,128)S(1)} %get-tuple-element.24.lower_ref, f32[17,136,128]{2,1,0:T(8,128)S(1)} %get-tuple-element.25.upper_ref), custom_call_target="tpu_custom_call" | custom-call | tf_op jit(solution)/shard_map/contour/pallas_call | solution.py:566
  106.8 0.0 all-to-all-done.1
  106.8 1.1 %copy_bitcast_fusion = f32[16,16,1024]{2,1,0:T(8,128)} fusion(f32[8,16,16,128]{3,2,1,0:T(8,128)S(1)} %all-to-all-done.1), kind=kLoop, calls=%fused_computation | loop fusion | bytes 2097152 | tf_op jit(solution)/shard_map/reshape | solution.py:565
  (1 shorter events, 0.0 us)
Async XLA Ops:
  0.6 8.1 %copy-start.1 = (f32[3]{0:T(128)S(1)}, f32[3]{0:T(128)}, u32[]{:S(2)}) copy-start(f32[3]{0:T(128)} %param.3) | copy-start | bytes 40
  0.6 1.2 %copy-start = (f32[16,16,1024]{2,1,0:T(8,128)S(1)}, f32[16,16,1024]{2,1,0:T(8,128)}, u32[]{:S(2)}) copy-start(f32[16,16,1024]{2,1,0:T(8,128)} %param.2) | copy-start | bytes 3145732
  3.4 23.7 %all-to-all-start = ((f32[8,2,152,128]{3,2,1,0:T(8,128)}), f32[8,2,152,128]{3,2,1,0:T(8,128)S(1)}, u32[]{:S(2)}, u32[]{:S(2)}) async-start(f32[8,2,152,128]{3,2,1,0:T(8,128)} %pack.1), calls=%async_computation | async-start | bytes 2490368 | tf_op jit(solution)/shard_map/all_to_all | solution.py:507
  28.0 19.6 %collective-permute-start.1 = (f32[8,152,128]{2,1,0:T(8,128)}, f32[8,152,128]{2,1,0:T(8,128)S(1)}, u32[]{:S(2)}, u32[]{:S(2)}) collective-permute-start(f32[8,152,128]{2,1,0:T(8,128)} %get-tuple-element.26), channel_id=1, source_target_pairs={{8,0},{16,8},{24,16},{32,24},{40,32},{48,40},{56,48},{64,56},{72,6... | collective-permute-start | bytes 1867784 | tf_op jit(solution)/shard_map/ppermute | solution.py:515
  29.6 18.0 %collective-permute-start = (f32[8,152,128]{2,1,0:T(8,128)S(1)}, f32[8,152,128]{2,1,0:T(8,128)S(1)}, u32[]{:S(2)}, u32[]{:S(2)}) collective-permute-start(f32[8,152,128]{2,1,0:T(8,128)S(1)} %get-tuple-element.27), channel_id=1, source_target_pairs={{0,8},{8,16},{16,24},{24,32},{32,40},{40,48},{48,56},{56,64},{64,7... | collective-permute-start | bytes 1867784 | tf_op jit(solution)/shard_map/ppermute | solution.py:514
  61.9 13.3 %collective-permute-start.3 = (f32[5,160,128]{2,1,0:T(8,128)S(1)}, f32[5,160,128]{2,1,0:T(8,128)S(1)}, u32[]{:S(2)}, u32[]{:S(2)}) collective-permute-start(f32[5,160,128]{2,1,0:T(8,128)S(1)} %get-tuple-element.17), channel_id=1, source_target_pairs={{8,0},{16,8},{24,16},{32,24},{40,32},{48,40},{56,48},{64,56},{72,6... | collective-permute-start | bytes 1228808 | tf_op jit(solution)/shard_map/ppermute | solution.py:538
  62.0 13.2 %collective-permute-start.2 = (f32[4,160,128]{2,1,0:T(8,128)S(1)}, f32[4,160,128]{2,1,0:T(8,128)S(1)}, u32[]{:S(2)}, u32[]{:S(2)}) collective-permute-start(f32[4,160,128]{2,1,0:T(8,128)S(1)} %get-tuple-element.16), channel_id=1, source_target_pairs={{0,8},{8,16},{16,24},{24,32},{32,40},{40,48},{48,56},{56,64},{64,7... | collective-permute-start | bytes 983048 | tf_op jit(solution)/shard_map/ppermute | solution.py:537
  85.9 20.9 %all-to-all-start.1 = ((f32[8,16,16,128]{3,2,1,0:T(8,128)}), f32[8,16,16,128]{3,2,1,0:T(8,128)S(1)}, u32[]{:S(2)}, u32[]{:S(2)}) async-start(f32[8,16,16,128]{3,2,1,0:T(8,128)} %get-tuple-element.23), calls=%async_computation.1 | async-start | bytes 2097152 | tf_op jit(solution)/shard_map/all_to_all | solution.py:564

commit v4 on v3

--- a/solution.py
+++ b/solution.py
@@ -230,7 +230,7 @@
     return first_x, last_x, first_z, last_z
 
 
-def inner_kernel(place_ref, scale_ref, u_ref, v_ref, w_ref, slots_ref, f0, f1):
+def inner_kernel(place_ref, scale_ref, u_ref, v_ref, w_ref, slots_ref, f0, f1, f2):
     count, halves, _, lanes = slots_ref.shape
     own = halves * count
     _, _, first_z, last_z = ends(place_ref)
@@ -243,13 +243,15 @@
     coefs = (u_ref, v_ref, w_ref)
     stage(f0, None, f1, coefs, scale_ref, EDGE + 3, own - 6, (0.0, 1.0))
     clamp_rows(f1, first_z, last_z, EDGE + 3, EDGE + own - 3, lanes)
+    stage(f1, f0, f2, coefs, scale_ref, EDGE + 6, own - 12, (0.75, 0.25))
+    clamp_rows(f2, first_z, last_z, EDGE + 6, EDGE + own - 6, lanes)
 
 
 def outer_kernel(
-    place_ref, scale_ref, u_ref, v_ref, w_ref, below_ref, above_ref, f0_in, f1_in,
+    place_ref, scale_ref, u_ref, v_ref, w_ref, below_ref, above_ref, f0_in, f1_in, f2_in,
     f0, f1, f2, up_ref, down_ref,
 ):
-    del f0_in, f1_in
+    del f0_in, f1_in, f2_in
     count, _, lanes = below_ref.shape
     begin, end = EDGE, f0.shape[0] - EDGE
     first_x, last_x, first_z, last_z = ends(place_ref)
@@ -282,9 +284,9 @@
     _, _, first_z, last_z = ends(place_ref)
     begin, end = EDGE, f0.shape[0] - EDGE
     coefs = (u_ref, v_ref, w_ref)
-    lo, hi = begin + HIGH, end - LOW
-    stage(f1, f0, f2, coefs, scale_ref, lo, hi - lo, (0.75, 0.25))
-    clamp_rows(f2, first_z, last_z, lo, hi, f2.shape[2])
+    for lo, hi in ((begin + HIGH, begin + 6), (end - 6, end - LOW)):
+        stage(f1, f0, f2, coefs, scale_ref, lo, hi - lo, (0.75, 0.25))
+        clamp_rows(f2, first_z, last_z, lo, hi, f2.shape[2])
     lo, hi = begin + 3, end - 3
     stage(f2, f0, f3, coefs, scale_ref, lo, hi - lo, (1.0 / 3.0, 2.0 / 3.0), LATE)
 
@@ -516,11 +518,11 @@
     planes = EDGE + own + EDGE
     field = pltpu.VMEM((planes, ROWS, wide), f32)
     coefs = [near(a) for a in (u, v, w)]
-    f0, f1 = pl.pallas_call(
+    f0, f1, f2 = pl.pallas_call(
         inner_kernel,
-        out_shape=[field, field],
+        out_shape=[field] * 3,
         in_specs=[SMEM, SMEM] + [VMEM] * 4,
-        out_specs=[VMEM] * 2,
+        out_specs=[VMEM] * 3,
         compiler_params=PARAMS,
         name="inner",
     )(place, scale, *coefs, near(slots))
@@ -528,12 +530,12 @@
         outer_kernel,
         out_shape=[field, field, field]
         + [pltpu.VMEM((n, ROWS, wide), f32) for n in (LOW, HIGH)],
-        in_specs=[SMEM, SMEM] + [VMEM] * 7,
+        in_specs=[SMEM, SMEM] + [VMEM] * 8,
         out_specs=[VMEM] * 5,
-        input_output_aliases={7: 0, 8: 1},
+        input_output_aliases={7: 0, 8: 1, 9: 2},
         compiler_params=PARAMS,
         name="outer",
-    )(place, scale, *coefs, near(below), near(above), near(f0), near(f1))
+    )(place, scale, *coefs, near(below), near(above), near(f0), near(f1), near(f2))
     below = lax.ppermute(up, "px", ring)
     above = lax.ppermute(down, "px", back_ring)
     f2, f3 = pl.pallas_call(

time: 109 us -> 109 us (level)
    pallas_call x1, Pallas kernels: 7.87 us -> 10.3 us  [shards(): pl.pallas_call(inner_kernel, out_shape=[field] * 3, in_specs=[SMEM, SMEM]...]
    ppermute x1, waiting for transfers between devices: 5.4 us -> 2.96 us  [shards(): above = lax.ppermute(slots[:, 0], 'px', back_ring)]
    pallas_call x1, Pallas kernels: 9.93 us -> 7.62 us  [shards(): pl.pallas_call(third_kernel, out_shape=[field, field], in_specs=[SMEM, SM...]
    ppermute x1, waiting for transfers between devices: 0.01 us -> 1.51 us  [shards(): above = lax.ppermute(down, 'px', back_ring)]
  transfers between devices with their start and end apart: 6 -> 6, of which waited for: 2 -> 3; matrix products, arithmetic and copies ran while one was open for 1% -> 1% of each run, Pallas kernels for 33% -> 33%
where the time goes in v4:
time: 109 us; the launch traced here: 107 us
  Pallas kernels  61.7 us (57%)
  waiting for transfers between devices  21.5 us (20%)
  starting transfers between devices  17 us (16%)
  local copies, waits for them, and re-layouts  3.83 us (4%)
  between operations  2.01 us (2%)
    pallas_call x1, Pallas kernels, shards(): pl.pallas_call(contour_kernel, out_shape=jax.ShapeDtypeStruct((3, own, wi...  17.3 us
    all_to_all x1, waiting for transfers between devices, shards(): slots = lax.all_to_all(slots, 'py', split_axis=0, concat_axis=0, tiled=True)  17 us
    pallas_call x1, Pallas kernels, shards(): pl.pallas_call(outer_kernel, out_shape=[field, field, field] + [pltpu.VME...  14.4 us
    pallas_call x1, Pallas kernels, shards(): pl.pallas_call(last_kernel, out_shape=[field, field, pltpu.VMEM((count_z,...  10.6 us
    pallas_call x1, Pallas kernels, shards(): pl.pallas_call(inner_kernel, out_shape=[field] * 3, in_specs=[SMEM, SMEM]...  10.3 us
    pallas_call x1, Pallas kernels, shards(): pl.pallas_call(third_kernel, out_shape=[field, field], in_specs=[SMEM, SM...  7.62 us
    all_to_all x1, starting transfers between devices, shards(): slots = lax.all_to_all(slots, 'py', split_axis=0, concat_axis=0, tiled=True)  5.37 us
    all_to_all x1, starting transfers between devices, shards(): back = lax.all_to_all(turned, 'py', split_axis=0, concat_axis=0, tiled=True)  3.56 us
  transfers between devices with their start and end apart: 6, of which 3 were waited for; matrix products, arithmetic and copies ran while one was open for 1% of the time, Pallas kernels for 33%

profile of v4, /device:TPU:9, one launch (start us, length us, event | category | flops | bytes accessed | tf_op | source)
XLA Modules:
  0.0 107.0 jit_solution(5432697961282982910)
XLA Ops:
  0.6 0.0 copy-start.1
  0.6 0.0 copy-start
  0.6 1.2 %copy-done = f32[16,16,1024]{2,1,0:T(8,128)S(1)} copy-done((f32[16,16,1024]{2,1,0:T(8,128)S(1)}, f32[16,16,1024]{2,1,0:T(8,128)}, u32[]{:S(2)}) %copy-start) | copy-done | bytes 1048600
  1.9 1.5 %pack.1 = f32[8,2,152,128]{3,2,1,0:T(8,128)} custom-call(f32[256,1024]{1,0:T(8,128)S(1)} %bitcast.20), custom_call_target="tpu_custom_call" | custom-call | tf_op jit(solution)/shard_map/pack/pallas_call | solution.py:500
  3.4 5.4 %all-to-all-start = ((f32[8,2,152,128]{3,2,1,0:T(8,128)}), f32[8,2,152,128]{3,2,1,0:T(8,128)S(1)}, u32[]{:S(2)}, u32[]{:S(2)}) async-start(f32[8,2,152,128]{3,2,1,0:T(8,128)} %pack.1), calls=%async_computation | async-start | bytes 2490368 | tf_op jit(solution)/shard_map/all_to_all | solution.py:509
  8.7 0.0 copy-done.1
  8.7 0.6 fusion
  10.0 0.1 broadcast_multiply_fusion.4
  10.0 0.1 sine_multiply_fusion.1
  10.1 17.0 %all-to-all-done.slots_ref = f32[8,2,152,128]{3,2,1,0:T(8,128)S(1)} async-done(((f32[8,2,152,128]{3,2,1,0:T(8,128)}), f32[8,2,152,128]{3,2,1,0:T(8,128)S(1)}, u32[]{:S(2)}, u32[]{:S(2)}) %all-to-all-start) | async-done | bytes 1245216 | tf_op jit(solution)/shard_map/all_to_all | solution.py:509
  27.1 0.9 slice_bitcast_fusion
  28.0 1.6 %collective-permute-start.1 = (f32[8,152,128]{2,1,0:T(8,128)}, f32[8,152,128]{2,1,0:T(8,128)S(1)}, u32[]{:S(2)}, u32[]{:S(2)}) collective-permute-start(f32[8,152,128]{2,1,0:T(8,128)} %get-tuple-element.28), channel_id=1, source_target_pairs={{8,0},{16,8},{24,16},{32,24},{40,32},{48,40},{56,48},{64,56},{72,6... | collective-permute-start | bytes 1867784 | tf_op jit(solution)/shard_map/ppermute | solution.py:517
  29.6 3.2 %collective-permute-start = (f32[8,152,128]{2,1,0:T(8,128)S(1)}, f32[8,152,128]{2,1,0:T(8,128)S(1)}, u32[]{:S(2)}, u32[]{:S(2)}) collective-permute-start(f32[8,152,128]{2,1,0:T(8,128)S(1)} %get-tuple-element.29), channel_id=1, source_target_pairs={{0,8},{8,16},{16,24},{24,32},{32,40},{40,48},{48,56},{56,64},{64,7... | collective-permute-start | bytes 1867784 | tf_op jit(solution)/shard_map/ppermute | solution.py:516
  32.8 0.1 pad_add_fusion.place_ref
  33.5 0.6 multiply_multiply_fusion
  34.1 0.1 sine_multiply_fusion
  34.2 0.1 broadcast_multiply_fusion.1
  34.3 10.3 %inner.1 = (f32[32,160,128]{2,1,0:T(8,128)S(1)}, f32[32,160,128]{2,1,0:T(8,128)S(1)}, f32[32,160,128]{2,1,0:T(8,128)S(1)}) custom-call(s32[4]{0:T(128)S(1)} %pad_add_fusion.place_ref, f32[3,32]{1,0:T(4,128)S(1)} %pad_maximum_fusion.scale_ref, f32[160,128]{1,0:T(8,128)S(1)} %get-tuple-element.31.u_ref, f32[160,128]{1,0:T(8,128)S(1)} %get-tuple-element.30.v_ref, ...), custom_call_target="tpu_custom_call" | custom-call | tf_op jit(solution)/shard_map/inner/pallas_call | solution.py:521
  44.6 3.0 %collective-permute-done.1.above_ref = f32[8,152,128]{2,1,0:T(8,128)S(1)} collective-permute-done((f32[8,152,128]{2,1,0:T(8,128)}, f32[8,152,128]{2,1,0:T(8,128)S(1)}, u32[]{:S(2)}, u32[]{:S(2)}) %collective-permute-start.1) | collective-permute-done | bytes 622624 | tf_op jit(solution)/shard_map/ppermute | solution.py:517
  47.6 0.0 collective-permute-done.below_ref
  47.6 14.4 %outer.1 = (f32[32,160,128]{2,1,0:T(8,128)S(1)}, f32[32,160,128]{2,1,0:T(8,128)S(1)}, f32[32,160,128]{2,1,0:T(8,128)S(1)}, f32[4,160,128]{2,1,0:T(8,128)S(1)}, f32[5,160,128]{2,1,0:T(8,128)S(1)}) custom-call(s32[4]{0:T(128)S(1)} %pad_add_fusion.place_ref, ...), custom_call_target="tpu_custom_call", output_to_operand_aliasing={{0}: (7, {}), {1}: (8, {}), {2}: (9, {})} | custom-call | tf_op jit(solution)/shard_map/outer/pallas_call | solution.py:529
  62.0 0.1 collective-permute-start.3
  62.1 3.2 %collective-permute-start.2 = (f32[4,160,128]{2,1,0:T(8,128)S(1)}, f32[4,160,128]{2,1,0:T(8,128)S(1)}, u32[]{:S(2)}, u32[]{:S(2)}) collective-permute-start(f32[4,160,128]{2,1,0:T(8,128)S(1)} %get-tuple-element.18), channel_id=1, source_target_pairs={{0,8},{8,16},{16,24},{24,32},{32,40},{40,48},{48,56},{56,64},{64,7... | collective-permute-start | bytes 983048 | tf_op jit(solution)/shard_map/ppermute | solution.py:539
  65.3 7.6 %third.1 = (f32[32,160,128]{2,1,0:T(8,128)S(1)}, f32[32,160,128]{2,1,0:T(8,128)S(1)}) custom-call(s32[4]{0:T(128)S(1)} %pad_add_fusion.place_ref, f32[3,32]{1,0:T(4,128)S(1)} %pad_maximum_fusion.scale_ref, f32[160,128]{1,0:T(8,128)S(1)} %get-tuple-element.31.u_ref, f32[160,128]{1,0:T(8,128)S(1)} %get-tuple-element.30.v_ref, ...), custom_call_target="tpu_custom_call", output_to_operand_aliasing={{0}: (7, {})} | custom-call | tf_op jit(solution)/shard_map/third/pallas_call | solution.py:541
  73.0 0.0 collective-permute-done.2.below_ref
  73.0 1.5 %collective-permute-done.3.above_ref = f32[5,160,128]{2,1,0:T(8,128)S(1)} collective-permute-done((f32[5,160,128]{2,1,0:T(8,128)S(1)}, f32[5,160,128]{2,1,0:T(8,128)S(1)}, u32[]{:S(2)}, u32[]{:S(2)}) %collective-permute-start.3) | collective-permute-done | bytes 409632 | tf_op jit(solution)/shard_map/ppermute | solution.py:540
  74.5 10.6 %last.1 = (f32[32,160,128]{2,1,0:T(8,128)S(1)}, f32[32,160,128]{2,1,0:T(8,128)S(1)}, f32[8,16,16,128]{3,2,1,0:T(8,128)}, f32[17,136,128]{2,1,0:T(8,128)S(1)}, f32[17,136,128]{2,1,0:T(8,128)S(1)}) custom-call(s32[4]{0:T(128)S(1)} %pad_add_fusion.place_ref, f32[3,32]{1,0:T(4,128)S(1)} %pad_maximum_fusion.scale_ref, ...), custom_call_target="tpu_custom_call", output_to_operand_aliasing={{0}: (8, {}), {1}: (9, {})} | custom-call | tf_op jit(solution)/shard_map/last/pallas_call | solution.py:550
  85.0 3.6 %all-to-all-start.1 = ((f32[8,16,16,128]{3,2,1,0:T(8,128)}), f32[8,16,16,128]{3,2,1,0:T(8,128)S(1)}, u32[]{:S(2)}, u32[]{:S(2)}) async-start(f32[8,16,16,128]{3,2,1,0:T(8,128)} %get-tuple-element.25), calls=%async_computation.1 | async-start | bytes 2097152 | tf_op jit(solution)/shard_map/all_to_all | solution.py:566
  88.6 17.3 %contour.1 = f32[3,16,128,128]{3,2,1,0:T(8,128)} custom-call(f32[17,136,128]{2,1,0:T(8,128)S(1)} %get-tuple-element.26.lower_ref, f32[17,136,128]{2,1,0:T(8,128)S(1)} %get-tuple-element.27.upper_ref), custom_call_target="tpu_custom_call" | custom-call | tf_op jit(solution)/shard_map/contour/pallas_call | solution.py:568
  105.9 0.0 all-to-all-done.1
  105.9 1.1 %copy_bitcast_fusion = f32[16,16,1024]{2,1,0:T(8,128)} fusion(f32[8,16,16,128]{3,2,1,0:T(8,128)S(1)} %all-to-all-done.1), kind=kLoop, calls=%fused_computation | loop fusion | bytes 2097152 | tf_op jit(solution)/shard_map/reshape | solution.py:567
  (1 shorter events, 0.0 us)
Async XLA Ops:
  0.6 8.1 %copy-start.1 = (f32[3]{0:T(128)S(1)}, f32[3]{0:T(128)}, u32[]{:S(2)}) copy-start(f32[3]{0:T(128)} %param.3) | copy-start | bytes 40
  0.6 1.2 %copy-start = (f32[16,16,1024]{2,1,0:T(8,128)S(1)}, f32[16,16,1024]{2,1,0:T(8,128)}, u32[]{:S(2)}) copy-start(f32[16,16,1024]{2,1,0:T(8,128)} %param.2) | copy-start | bytes 3145732
  3.4 23.7 %all-to-all-start = ((f32[8,2,152,128]{3,2,1,0:T(8,128)}), f32[8,2,152,128]{3,2,1,0:T(8,128)S(1)}, u32[]{:S(2)}, u32[]{:S(2)}) async-start(f32[8,2,152,128]{3,2,1,0:T(8,128)} %pack.1), calls=%async_computation | async-start | bytes 2490368 | tf_op jit(solution)/shard_map/all_to_all | solution.py:509
  28.0 19.6 %collective-permute-start.1 = (f32[8,152,128]{2,1,0:T(8,128)}, f32[8,152,128]{2,1,0:T(8,128)S(1)}, u32[]{:S(2)}, u32[]{:S(2)}) collective-permute-start(f32[8,152,128]{2,1,0:T(8,128)} %get-tuple-element.28), channel_id=1, source_target_pairs={{8,0},{16,8},{24,16},{32,24},{40,32},{48,40},{56,48},{64,56},{72,6... | collective-permute-start | bytes 1867784 | tf_op jit(solution)/shard_map/ppermute | solution.py:517
  29.6 18.0 %collective-permute-start = (f32[8,152,128]{2,1,0:T(8,128)S(1)}, f32[8,152,128]{2,1,0:T(8,128)S(1)}, u32[]{:S(2)}, u32[]{:S(2)}) collective-permute-start(f32[8,152,128]{2,1,0:T(8,128)S(1)} %get-tuple-element.29), channel_id=1, source_target_pairs={{0,8},{8,16},{16,24},{24,32},{32,40},{40,48},{48,56},{56,64},{64,7... | collective-permute-start | bytes 1867784 | tf_op jit(solution)/shard_map/ppermute | solution.py:516
  62.0 12.5 %collective-permute-start.3 = (f32[5,160,128]{2,1,0:T(8,128)S(1)}, f32[5,160,128]{2,1,0:T(8,128)S(1)}, u32[]{:S(2)}, u32[]{:S(2)}) collective-permute-start(f32[5,160,128]{2,1,0:T(8,128)S(1)} %get-tuple-element.19), channel_id=1, source_target_pairs={{8,0},{16,8},{24,16},{32,24},{40,32},{48,40},{56,48},{64,56},{72,6... | collective-permute-start | bytes 1228808 | tf_op jit(solution)/shard_map/ppermute | solution.py:540
  62.1 10.9 %collective-permute-start.2 = (f32[4,160,128]{2,1,0:T(8,128)S(1)}, f32[4,160,128]{2,1,0:T(8,128)S(1)}, u32[]{:S(2)}, u32[]{:S(2)}) collective-permute-start(f32[4,160,128]{2,1,0:T(8,128)S(1)} %get-tuple-element.18), channel_id=1, source_target_pairs={{0,8},{8,16},{16,24},{24,32},{32,40},{40,48},{48,56},{56,64},{64,7... | collective-permute-start | bytes 983048 | tf_op jit(solution)/shard_map/ppermute | solution.py:539
  85.0 20.9 %all-to-all-start.1 = ((f32[8,16,16,128]{3,2,1,0:T(8,128)}), f32[8,16,16,128]{3,2,1,0:T(8,128)S(1)}, u32[]{:S(2)}, u32[]{:S(2)}) async-start(f32[8,16,16,128]{3,2,1,0:T(8,128)} %get-tuple-element.25), calls=%async_computation.1 | async-start | bytes 2097152 | tf_op jit(solution)/shard_map/all_to_all | solution.py:566
